TPU v7x, 32 devices: a whole 2x2x4 slice. The times are simulated.
32 devices in a mesh: visit: 8 (over z, y), tile: 4 (over x, core).
Axes of the slice: x: 2, y: 2, z: 4, core: 2. Of those that a mesh axis runs over, the one named last changes fastest.
Arguments:
- science: float32 [8, 256, 4096], P('visit', 'tile'), may hold values from -8 to 8
- science_var: float32 [8, 256, 4096], P('visit', 'tile'), may hold values from 0.5 to 4
- template: float32 [8, 256, 4096], P('visit', 'tile'), may hold values from -8 to 8
- template_var: float32 [8, 256, 4096], P('visit', 'tile'), may hold values from 0.1 to 1
- intersection: int32 [8, 32, 1], replicated, may hold values from 0 to 7; in each aligned block of 32 rows (0 to 31, 32 to 63, ..., all dimensions but the last counted through in order) at most 4 rows name the same one
- col_offset: int32 [8, 32], replicated, may hold values from 0 to 3968
- basis_row: float32 [16, 41], replicated, may hold values from -1 to 1
- basis_col: float32 [16, 41], replicated, may hold values from -1 to 1
- coef_sets: float32 [8, 16], replicated, may hold values from -1.5 to 1.5
- tile_coef: int32 [8, 4], replicated, may hold values from 0 to 7
Outputs:
- difference: float32 [8, 256, 4096], P('visit', 'tile')
- difference_var: float32 [8, 256, 4096], P('visit', 'tile')
Inputs may be any that keep to these rules, and one draw needn't show every extreme that they name: `intersection`: no visit takes more than 4 of its 32 pieces from one owner, and some visit takes exactly 4 from one owner.
All inputs are finite; a program needn't handle non-finite values.
Results may differ from a plain program's by a relative error of at most 0.0003.
Values sent between devices are 32-bit elements; how exact they have to be, the bound alone decides.
No kernel may reach another device: no remote copies, remote signals or barrier semaphores. Data moves between devices by JAX's collectives and lax.ppermute only.
A program may use at most 320 MiB of HBM per device.

v0:
```python
import functools

import jax
import jax.numpy as jnp
from jax import lax
from jax.experimental import pallas as pl
from jax.experimental.pallas import tpu as pltpu
from jax.sharding import PartitionSpec as P


PIECE = 128
GROUP = 11
SUB = 16
BLOCK = 256


SMEM = pltpu.MemorySpace.SMEM
VMEM = pltpu.MemorySpace.VMEM


def partner(me, step, count):
    if count & (count - 1) == 0:
        return me ^ step
    return lax.rem(me + step, count)


def sender(me, step, count):
    if count & (count - 1) == 0:
        return me ^ step
    return lax.rem(me + count - step, count)


def pairs(step, count):
    if count & (count - 1) == 0:
        return [(i, i ^ step) for i in range(count)]
    return [(i, (i + step) % count) for i in range(count)]


def cut_kernel(count, slots, pieces, me_ref, owner_ref, offset_ref, strip_ref, *rest):
    outs, (strip, cuts, starts, strip_sem, out_sems) = rest[:count], rest[count:]
    me = me_ref[0]
    rows, width = strip.shape
    last = width // PIECE - 1
    load = pltpu.make_async_copy(strip_ref, strip, strip_sem)
    load.start()
    for step in range(count):
        visit = partner(me, step, count)
        begin = step * (slots + 1)
        for slot in range(slots):
            starts[begin + slot] = 0
        found = jnp.int32(begin)
        for k in range(pieces):
            starts[found] = offset_ref[visit, k]
            found = found + (owner_ref[visit, k] == me).astype(jnp.int32)
    load.wait()
    lane = lax.broadcasted_iota(jnp.int32, (rows, PIECE), 1)
    stores = []
    for step in range(count):
        for slot in range(slots):
            start = starts[step * (slots + 1) + slot]
            block = start // PIECE
            shift = lax.rem(start, PIECE)
            after = jnp.minimum(block + 1, last)
            left = strip[:, pl.ds(pl.multiple_of(block * PIECE, PIECE), PIECE)]
            right = strip[:, pl.ds(pl.multiple_of(after * PIECE, PIECE), PIECE)]
            joined = jnp.where(lane < shift, right, left)
            cuts[step, slot] = pltpu.roll(joined, lax.rem(PIECE - shift, PIECE), 1)
        store = pltpu.make_async_copy(cuts.at[step], outs[step], out_sems.at[step])
        store.start()
        stores.append(store)
    for store in stores:
        store.wait()


def cut(me, owners, offsets, strip, count, slots):
    pieces = owners.shape[1]
    rows, width = strip.shape
    shape = jax.ShapeDtypeStruct((slots, rows, PIECE), jnp.float32)
    return pl.pallas_call(
        functools.partial(cut_kernel, count, slots, pieces),
        out_shape=[shape] * count,
        in_specs=[pl.BlockSpec(memory_space=SMEM)] * 3 + [pl.BlockSpec(memory_space=pl.ANY)],
        out_specs=[pl.BlockSpec(memory_space=pl.ANY)] * count,
        scratch_shapes=[
            pltpu.VMEM((rows, width), jnp.float32),
            pltpu.VMEM((count, slots, rows, PIECE), jnp.float32),
            pltpu.SMEM((count * (slots + 1),), jnp.int32),
            pltpu.SemaphoreType.DMA,
            pltpu.SemaphoreType.DMA((count,)),
        ],
        cost_estimate=pl.CostEstimate(flops=0, transcendentals=0, bytes_accessed=2 * strip.size * 4),
        name="cut",
    )(me, owners, offsets, strip)


def find_places(count, slots, pieces, me, owner_ref, place, seen):
    for owner in range(count):
        seen[owner] = 0
    for entry in range(count * slots):
        place[entry] = -1

    def find(k, carry):
        owner = owner_ref[me, k]
        nth = seen[owner]
        place[owner * slots + nth] = k
        seen[owner] = nth + 1
        return carry

    lax.fori_loop(0, pieces, find, jnp.int32(0), unroll=8)


def when_taken(count, slots, pieces, k, body):
    if count * slots == pieces:
        body()
    else:
        pl.when(k >= 0)(body)


def at_piece(k):
    return pl.ds(pl.multiple_of(k * PIECE, PIECE), PIECE)


def each_slot(count, slots, me, place):
    for step in range(count):
        owner = sender(me, step, count)
        for slot in range(slots):
            yield step, slot, place[owner * slots + slot]


def places_scratch(count, slots):
    return [pltpu.SMEM((count * slots,), jnp.int32), pltpu.SMEM((count,), jnp.int32)]


def edges_kernel(count, slots, pieces, reach, me_ref, owner_ref, *rest):
    blocks = rest[:count]
    head_ref, tail_ref, place, seen = rest[count:]
    me = me_ref[0]
    rows = blocks[0].shape[1]
    find_places(count, slots, pieces, me, owner_ref, place, seen)
    for position, slot, k in each_slot(count, slots, me, place):

        def put(position=position, slot=slot, k=k):
            head_ref[:, at_piece(k)] = blocks[position][slot, :reach]
            tail_ref[:, at_piece(k)] = blocks[position][slot, rows - reach :]

        when_taken(count, slots, pieces, k, put)


def edges(me, owners, blocks, width, reach):
    count, pieces = len(blocks), owners.shape[1]
    slots = blocks[0].shape[0]
    shape = jax.ShapeDtypeStruct((reach, width), jnp.float32)
    return pl.pallas_call(
        functools.partial(edges_kernel, count, slots, pieces, reach),
        out_shape=[shape, shape],
        in_specs=[pl.BlockSpec(memory_space=SMEM)] * 2 + [pl.BlockSpec(memory_space=VMEM)] * count,
        out_specs=[pl.BlockSpec(memory_space=VMEM)] * 2,
        scratch_shapes=places_scratch(count, slots),
        cost_estimate=pl.CostEstimate(flops=0, transcendentals=0, bytes_accessed=4 * reach * width * 4),
        compiler_params=pltpu.CompilerParams(vmem_limit_bytes=6 << 20),
        name="edges",
    )(me, owners, *blocks)


def spread_kernel(count, slots, pieces, me_ref, owner_ref, power_ref, science_ref, *rest):
    blocks = rest[:count]
    out_ref, place, seen = rest[count:]
    me = me_ref[0]
    power = power_ref[0]
    find_places(count, slots, pieces, me, owner_ref, place, seen)
    for position, slot, k in each_slot(count, slots, me, place):

        def put(position=position, slot=slot, k=k):
            out_ref[:, at_piece(k)] = science_ref[:, at_piece(k)] + power * blocks[position][slot]

        when_taken(count, slots, pieces, k, put)


def spread(me, owners, power, science_var, blocks):
    count, pieces = len(blocks), owners.shape[1]
    slots = blocks[0].shape[0]
    size = science_var.size
    return pl.pallas_call(
        functools.partial(spread_kernel, count, slots, pieces),
        out_shape=jax.ShapeDtypeStruct(science_var.shape, jnp.float32),
        in_specs=[pl.BlockSpec(memory_space=SMEM)] * 3 + [pl.BlockSpec(memory_space=VMEM)] * (1 + count),
        out_specs=pl.BlockSpec(memory_space=VMEM),
        scratch_shapes=places_scratch(count, slots),
        cost_estimate=pl.CostEstimate(flops=2 * size, transcendentals=0, bytes_accessed=3 * size * 4),
        compiler_params=pltpu.CompilerParams(vmem_limit_bytes=6 << 20),
        name="spread",
    )(me, owners, power, science_var, *blocks)


def split(x):
    high = x.astype(jnp.bfloat16)
    return high, (x - high.astype(jnp.float32)).astype(jnp.bfloat16)


def band_kernel(taps_ref, both_ref):
    deep = taps_ref.shape[1]
    half = both_ref.shape[0] // 2
    for q in range(GROUP):
        for at in range(0, deep, PIECE):
            line = jnp.broadcast_to(taps_ref[q : q + 1, at : at + PIECE], (SUB, PIECE))
            high, low = split(pltpu.roll(line, 0, 1, stride=1, stride_axis=0))
            both_ref[q * SUB : (q + 1) * SUB, at : at + PIECE] = high
            both_ref[half + q * SUB : half + (q + 1) * SUB, at : at + PIECE] = low


def bands(taps, window, lead):
    side = taps.shape[0]
    shifts = -(-side // GROUP)
    taps = jnp.pad(taps, ((0, shifts * GROUP - side), (lead, window - lead - side)))
    taps = taps.reshape(shifts, GROUP, window).transpose(1, 0, 2).reshape(GROUP, shifts * window)
    deep = -(-shifts * window // PIECE) * PIECE
    taps = jnp.pad(taps, ((0, 0), (0, deep - shifts * window)))
    return pl.pallas_call(
        band_kernel,
        out_shape=jax.ShapeDtypeStruct((2 * GROUP * SUB, deep), jnp.bfloat16),
        in_specs=[pl.BlockSpec(memory_space=VMEM)],
        out_specs=pl.BlockSpec(memory_space=VMEM),
        cost_estimate=pl.CostEstimate(flops=0, transcendentals=0, bytes_accessed=4 * GROUP * SUB * deep),
        compiler_params=pltpu.CompilerParams(vmem_limit_bytes=4 << 20),
        name="bands",
    )(taps)


def turn(x, lanes):
    return pltpu.roll(x, PIECE - lanes, 1)


def match_kernel(margin, shifts, count, slots, pieces, me_ref, owner_ref, both_ref, above_ref, below_ref, science_ref, *rest):
    images, out_ref, rest = rest[:count], rest[count], rest[count + 1 :]
    place, seen, wide, high0, high1, low0, low1, part0, part1, kept_image, kept_part = rest
    rows, width = science_ref.shape
    reach = above_ref.shape[0]
    window = SUB + 2 * reach
    filled = rows + 2 * reach
    half = both_ref.shape[0] // 2
    high, low, part = (high0, high1), (low0, low1), (part0, part1)
    me = me_ref[0]
    find_places(count, slots, pieces, me, owner_ref, place, seen)
    for position, slot, k in each_slot(count, slots, me, place):

        def put(position=position, slot=slot, k=k):
            wide[reach : reach + rows, at_piece(k + 1)] = images[position][slot]

        when_taken(count, slots, pieces, k, put)
    wide[:, 0:PIECE] = jnp.zeros((filled, PIECE), jnp.float32)
    wide[:, PIECE + width :] = jnp.zeros((filled, wide.shape[1] - PIECE - width), jnp.float32)
    wide[0:reach, PIECE : PIECE + width] = above_ref[...]
    wide[reach + rows :, PIECE : PIECE + width] = below_ref[...]
    blocks = width // BLOCK
    lane_image = lax.broadcasted_iota(jnp.int32, (filled, PIECE), 1)
    lane_part = lax.broadcasted_iota(jnp.int32, (SUB, PIECE), 1)

    def build(b, parity, first=False):
        begin = b * BLOCK
        for m in range(shifts):
            offset = PIECE - margin + m * GROUP
            lanes = offset % PIECE
            at = begin + offset - lanes
            span = slice(m * filled, (m + 1) * filled)

            def column(k, at=at):
                return wide[:, pl.ds(pl.multiple_of(at + k * PIECE, PIECE), PIECE)]

            if lanes:
                turned = [turn(column(0), lanes) if first else kept_image[span, :]]
                turned += [turn(column(k), lanes) for k in (1, 2)]
                kept_image[span, :] = turned[2]
                mask = lane_image < PIECE - lanes
                parts = [jnp.where(mask, turned[k], turned[k + 1]) for k in (0, 1)]
            else:
                parts = [column(0), column(1)]
            for k in (0, 1):
                near, rest = split(parts[k])
                high[parity][span, k * PIECE : (k + 1) * PIECE] = near
                low[parity][span, k * PIECE : (k + 1) * PIECE] = rest

    def multiply(parity, columns=BLOCK):
        for top in range(0, rows, SUB):
            spans = [slice(m * filled + top, m * filled + top + window) for m in range(shifts)]
            near = jnp.concatenate([high[parity][span, :columns] for span in spans], axis=0)
            rest = jnp.concatenate([low[parity][span, :columns] for span in spans], axis=0)
            deep = near.shape[0]
            product = jnp.dot(both_ref[:half, :deep], rest, preferred_element_type=jnp.float32)
            pair = jnp.dot(both_ref[:, :deep], near, preferred_element_type=jnp.float32)
            part[parity][top * GROUP : (top + SUB) * GROUP, :columns] = product + (pair[:half] + pair[half:])

    def keep():
        for first in range(0, rows * GROUP, SUB):
            q = first // SUB % GROUP
            if q:
                kept_part[first : first + SUB, :] = turn(part0[first : first + SUB, :PIECE], q)

    def join(b, parity):
        here, after = part[parity], part[1 - parity]
        begin = pl.multiple_of(b * BLOCK, BLOCK)
        for top in range(0, rows, SUB):
            span = slice(top * GROUP, top * GROUP + SUB)
            totals = [here[span, :PIECE], here[span, PIECE:]]
            for q in range(1, GROUP):
                span = slice(top * GROUP + q * SUB, top * GROUP + (q + 1) * SUB)
                turned = [kept_part[span, :], turn(here[span, PIECE:], q), turn(after[span, :PIECE], q)]
                kept_part[span, :] = turned[2]
                for k in (0, 1):
                    totals[k] = totals[k] + jnp.where(lane_part < PIECE - q, turned[k], turned[k + 1])
            for k in (0, 1):
                at = pl.ds(pl.multiple_of(begin + k * PIECE, PIECE), PIECE)
                out_ref[top : top + SUB, at] = science_ref[top : top + SUB, at] - totals[k]

    build(0, 0, first=True)
    build(1, 1)
    multiply(0)
    keep()
    build(2, 0)
    multiply(1)

    @pl.loop(1, blocks // 2)
    def _(p):
        b = p * 2
        join(b - 2, 0)
        build(b + 1, 1)
        multiply(0)
        join(b - 1, 1)
        build(b + 2, 0)
        multiply(1)

    join(blocks - 2, 0)
    multiply(0, PIECE)
    join(blocks - 1, 1)


def match(margin, shifts, me, owners, both, above, below, science, images):
    rows, width = science.shape
    count, pieces = len(images), owners.shape[1]
    slots = images[0].shape[0]
    reach = above.shape[0]
    filled = rows + 2 * reach
    return pl.pallas_call(
        functools.partial(match_kernel, margin, shifts, count, slots, pieces),
        out_shape=jax.ShapeDtypeStruct(science.shape, jnp.float32),
        in_specs=[pl.BlockSpec(memory_space=SMEM)] * 2
        + [pl.BlockSpec(memory_space=VMEM)] * (4 + count),
        out_specs=pl.BlockSpec(memory_space=VMEM),
        scratch_shapes=places_scratch(count, slots)
        + [
            pltpu.VMEM((filled, width + BLOCK + 2 * PIECE), jnp.float32),
            *[pltpu.VMEM((shifts * filled, BLOCK), jnp.bfloat16)] * 4,
            *[pltpu.VMEM((GROUP * rows, BLOCK), jnp.float32)] * 2,
            pltpu.VMEM((shifts * filled, PIECE), jnp.float32),
            pltpu.VMEM((GROUP * rows, PIECE), jnp.float32),
        ],
        cost_estimate=pl.CostEstimate(
            flops=6 * GROUP * rows * both.shape[1] * width, transcendentals=0, bytes_accessed=4 * rows * width * 4
        ),
        compiler_params=pltpu.CompilerParams(vmem_limit_bytes=20 << 20),
        name="match",
    )(me, owners, both, above, below, science, *images)


def local(
    science,
    science_var,
    template,
    template_var,
    intersection,
    col_offset,
    basis_row,
    basis_col,
    coef_sets,
    tile_coef,
):
    count = lax.axis_size("visit")
    pieces = intersection.shape[1]
    slots = max(2, pieces // count)
    _, width = science.shape[1:]
    side = basis_row.shape[1]
    margin = (side - 1) // 2
    reach = -(-margin // 8) * 8
    me = lax.axis_index("visit")
    tile_me = lax.axis_index("tile")
    highest = lax.Precision.HIGHEST
    me_ref = me.astype(jnp.int32).reshape(1)
    owners = intersection[:, :, 0]
    mine = cut(me_ref, owners, col_offset, template[0], count, slots)
    got = [mine[0]] + [None] * (count - 1)
    for step in steps(count):
        got[step] = lax.ppermute(mine[step], "visit", pairs(step, count))
    mine_var = cut(me_ref, owners, col_offset, template_var[0], count, slots)
    got_var = [mine_var[0]] + [None] * (count - 1)
    for step in steps(count):
        got_var[step] = lax.ppermute(mine_var[step], "visit", pairs(step, count))

    chosen = lax.dynamic_slice(tile_coef, (me, tile_me), (1, 1))[0, 0]
    coeffs = lax.dynamic_index_in_dim(coef_sets, chosen, 0, keepdims=False)
    taps = jnp.einsum("bc,ba->ca", coeffs[:, None] * basis_col, basis_row, precision=highest)
    power = jnp.sum(taps * taps).reshape(1)
    both = bands(taps, SUB + 2 * reach, reach - margin)

    head, tail = edges(me_ref, owners, got, width, reach)
    tiles = lax.axis_size("tile")
    above = lax.ppermute(tail, "tile", [(i, i + 1) for i in range(tiles - 1)])
    below = lax.ppermute(head, "tile", [(i + 1, i) for i in range(tiles - 1)])
    shifts = -(-side // GROUP)
    difference = match(margin, shifts, me_ref, owners, both, above, below, science[0], got)
    difference_var = spread(me_ref, owners, power, science_var[0], got_var)
    return difference[None], difference_var[None]


def steps(count):
    return sorted(range(1, count), key=lambda step: -(step.bit_length()))


def solution(mesh):
    split_spec = P("visit", "tile", None)
    return jax.shard_map(
        local,
        mesh=mesh,
        in_specs=(split_spec,) * 4 + (P(),) * 6,
        out_specs=(split_spec, split_spec),
        check_vma=False,
    )
```

profile of v0, /device:TPU:11, one launch (start us, length us, event | category | flops | bytes accessed | tf_op | source)
XLA Modules:
  0.0 81.5 jit_solution(8867801686741535560)
XLA Ops:
  0.7 3.2 %cut.2 = (f32[4,64,128]{2,1,0:T(8,128)}, f32[4,64,128]{2,1,0:T(8,128)}, f32[4,64,128]{2,1,0:T(8,128)}, f32[4,64,128]{2,1,0:T(8,128)}, f32[4,64,128]{2,1,0:T(8,12...) custom-call(s32[1]{0:T(128)} %bitcast.me_ref, s32[8,32]{1,0:T(8,128)} %bitcast.15, ...), custom_call_target="tpu_custom_call" | custom-call | bytes 2097152 | tf_op jit(solution)/shard_map/cut/pallas_call | solution.py:79
  3.8 1.3 %collective-permute-start = (f32[4,64,128]{2,1,0:T(8,128)}, f32[4,64,128]{2,1,0:T(8,128)S(1)}, u32[]{:S(2)}, u32[]{:S(2)}) collective-permute-start(f32[4,64,128]{2,1,0:T(8,128)} %get-tuple-element.21), channel_id=1, source_target_pairs={{0,4},{4,0},{8,12},{12,8},{16,20},{20,16},{24,28},{28,24},{1,5},{5... | collective-permute-start | bytes 393224 | tf_op jit(solution)/shard_map/ppermute | solution.py:391
  5.3 1.2 %collective-permute-start.2 = (f32[4,64,128]{2,1,0:T(8,128)}, f32[4,64,128]{2,1,0:T(8,128)S(1)}, u32[]{:S(2)}, u32[]{:S(2)}) collective-permute-start(f32[4,64,128]{2,1,0:T(8,128)} %get-tuple-element.23), channel_id=1, source_target_pairs={{0,12},{4,8},{8,4},{12,0},{16,28},{20,24},{24,20},{28,16},{1,13},{... | collective-permute-start | bytes 393224 | tf_op jit(solution)/shard_map/ppermute | solution.py:391
  6.5 2.3 %collective-permute-start.3 = (f32[4,64,128]{2,1,0:T(8,128)}, f32[4,64,128]{2,1,0:T(8,128)S(1)}, u32[]{:S(2)}, u32[]{:S(2)}) collective-permute-start(f32[4,64,128]{2,1,0:T(8,128)} %get-tuple-element.24), channel_id=1, source_target_pairs={{0,16},{4,20},{8,24},{12,28},{16,0},{20,4},{24,8},{28,12},{1,17},{... | collective-permute-start | bytes 393224 | tf_op jit(solution)/shard_map/ppermute | solution.py:391
  8.8 1.0 %collective-permute-start.4 = (f32[4,64,128]{2,1,0:T(8,128)}, f32[4,64,128]{2,1,0:T(8,128)S(1)}, u32[]{:S(2)}, u32[]{:S(2)}) collective-permute-start(f32[4,64,128]{2,1,0:T(8,128)} %get-tuple-element.25), channel_id=1, source_target_pairs={{0,20},{4,16},{8,28},{12,24},{16,4},{20,0},{24,12},{28,8},{1,21},{... | collective-permute-start | bytes 393224 | tf_op jit(solution)/shard_map/ppermute | solution.py:391
  9.9 1.3 %collective-permute-start.5 = (f32[4,64,128]{2,1,0:T(8,128)}, f32[4,64,128]{2,1,0:T(8,128)S(1)}, u32[]{:S(2)}, u32[]{:S(2)}) collective-permute-start(f32[4,64,128]{2,1,0:T(8,128)} %get-tuple-element.26), channel_id=1, source_target_pairs={{0,24},{4,28},{8,16},{12,20},{16,8},{20,12},{24,0},{28,4},{1,25},{... | collective-permute-start | bytes 393224 | tf_op jit(solution)/shard_map/ppermute | solution.py:391
  11.3 3.3 %cut.3 = (f32[4,64,128]{2,1,0:T(8,128)}, f32[4,64,128]{2,1,0:T(8,128)}, f32[4,64,128]{2,1,0:T(8,128)}, f32[4,64,128]{2,1,0:T(8,128)}, f32[4,64,128]{2,1,0:T(8,12...) custom-call(s32[1]{0:T(128)} %bitcast.me_ref, s32[8,32]{1,0:T(8,128)} %bitcast.16, ...), custom_call_target="tpu_custom_call" | custom-call | bytes 2097152 | tf_op jit(solution)/shard_map/cut/pallas_call | solution.py:79
  14.6 1.3 %collective-permute-start.9 = (f32[4,64,128]{2,1,0:T(8,128)}, f32[4,64,128]{2,1,0:T(8,128)S(1)}, u32[]{:S(2)}, u32[]{:S(2)}) collective-permute-start(f32[4,64,128]{2,1,0:T(8,128)} %get-tuple-element.31), channel_id=1, source_target_pairs={{0,4},{4,0},{8,12},{12,8},{16,20},{20,16},{24,28},{28,24},{1,5},{5... | collective-permute-start | bytes 393224 | tf_op jit(solution)/shard_map/ppermute | solution.py:395
  15.9 8.7 %collective-permute-done.4.rest_5_ = f32[4,64,128]{2,1,0:T(8,128)S(1)} collective-permute-done((f32[4,64,128]{2,1,0:T(8,128)}, f32[4,64,128]{2,1,0:T(8,128)S(1)}, u32[]{:S(2)}, u32[]{:S(2)}) %collective-permute-start.4) | collective-permute-done | bytes 131104 | tf_op jit(solution)/shard_map/ppermute | solution.py:391
  24.6 3.7 %collective-permute-done.5.rest_6_ = f32[4,64,128]{2,1,0:T(8,128)S(1)} collective-permute-done((f32[4,64,128]{2,1,0:T(8,128)}, f32[4,64,128]{2,1,0:T(8,128)S(1)}, u32[]{:S(2)}, u32[]{:S(2)}) %collective-permute-start.5) | collective-permute-done | bytes 131104 | tf_op jit(solution)/shard_map/ppermute | solution.py:391
  28.3 3.9 %collective-permute-done.6.rest_7_ = f32[4,64,128]{2,1,0:T(8,128)S(1)} collective-permute-done((f32[4,64,128]{2,1,0:T(8,128)}, f32[4,64,128]{2,1,0:T(8,128)S(1)}, u32[]{:S(2)}, u32[]{:S(2)}) %collective-permute-start.6) | collective-permute-done | bytes 131104 | tf_op jit(solution)/shard_map/ppermute | solution.py:391
  32.3 1.8 %edges.1 = (f32[24,4096]{1,0:T(8,128)}, f32[24,4096]{1,0:T(8,128)}) custom-call(s32[1]{0:T(128)} %bitcast.me_ref, s32[8,32]{1,0:T(8,128)S(1)} %bitcast.17, f32[4,64,128]{2,1,0:T(8,128)S(1)} %copy-done.3, f32[4,64,128]{2,1,0:T(8,128)S(1)} %collective-permute-done.rest_1_, f32[4,64,128]{2,1,0:T(8,128)S(1)} %collective-permute-done.1.rest_2_, ...), custom_call_target="tpu_custom_call" | custom-call | bytes 1572864 | tf_op jit(solution)/shard_map/edges/pallas_call | solution.py:153
  34.0 1.3 %collective-permute-start.7 = (f32[24,4096]{1,0:T(8,128)}, f32[24,4096]{1,0:T(8,128)}, u32[]{:S(2)}, u32[]{:S(2)}) collective-permute-start(f32[24,4096]{1,0:T(8,128)} %get-tuple-element.28), channel_id=1, source_target_pairs={{0,1},{1,2},{2,3},{4,5},{5,6},{6,7},{8,9},{9,10},{10,11},{12,13},{... | collective-permute-start | bytes 1179656 | tf_op jit(solution)/shard_map/ppermute | solution.py:405
  35.3 4.8 %collective-permute-start.8 = (f32[24,4096]{1,0:T(8,128)}, f32[24,4096]{1,0:T(8,128)}, u32[]{:S(2)}, u32[]{:S(2)}) collective-permute-start(f32[24,4096]{1,0:T(8,128)} %get-tuple-element.29), channel_id=1, source_target_pairs={{1,0},{2,1},{3,2},{5,4},{6,5},{7,6},{9,8},{10,9},{11,10},{13,12},{... | collective-permute-start | bytes 1179656 | tf_op jit(solution)/shard_map/ppermute | solution.py:406
  40.1 1.4 %collective-permute-start.11 = (f32[4,64,128]{2,1,0:T(8,128)}, f32[4,64,128]{2,1,0:T(8,128)S(1)}, u32[]{:S(2)}, u32[]{:S(2)}) collective-permute-start(f32[4,64,128]{2,1,0:T(8,128)} %get-tuple-element.33), channel_id=1, source_target_pairs={{0,12},{4,8},{8,4},{12,0},{16,28},{20,24},{24,20},{28,16},{1,13},{... | collective-permute-start | bytes 393224 | tf_op jit(solution)/shard_map/ppermute | solution.py:395
  41.5 1.6 %collective-permute-start.12 = (f32[4,64,128]{2,1,0:T(8,128)}, f32[4,64,128]{2,1,0:T(8,128)S(1)}, u32[]{:S(2)}, u32[]{:S(2)}) collective-permute-start(f32[4,64,128]{2,1,0:T(8,128)} %get-tuple-element.34), channel_id=1, source_target_pairs={{0,16},{4,20},{8,24},{12,28},{16,0},{20,4},{24,8},{28,12},{1,17},{... | collective-permute-start | bytes 393224 | tf_op jit(solution)/shard_map/ppermute | solution.py:395
  43.1 1.3 %dynamic_slice.7 = s32[1,1]{0,1:T(1,128)} dynamic-slice(s32[8,4]{0,1:T(4,128)} %param.19, s32[]{:T(128)S(6)} %select_n.10, s32[]{:T(128)S(6)} %select_n.11), dynamic_slice_sizes={1,1} | dynamic-slice | bytes 12 | tf_op jit(solution)/shard_map/dynamic_slice | solution.py:397
  47.0 1.7 %collective-permute-start.13 = (f32[4,64,128]{2,1,0:T(8,128)}, f32[4,64,128]{2,1,0:T(8,128)S(1)}, u32[]{:S(2)}, u32[]{:S(2)}) collective-permute-start(f32[4,64,128]{2,1,0:T(8,128)} %get-tuple-element.35), channel_id=1, source_target_pairs={{0,20},{4,16},{8,28},{12,24},{16,4},{20,0},{24,12},{28,8},{1,21},{... | collective-permute-start | bytes 393224 | tf_op jit(solution)/shard_map/ppermute | solution.py:395
  48.8 1.8 %collective-permute-start.14 = (f32[4,64,128]{2,1,0:T(8,128)}, f32[4,64,128]{2,1,0:T(8,128)S(1)}, u32[]{:S(2)}, u32[]{:S(2)}) collective-permute-start(f32[4,64,128]{2,1,0:T(8,128)} %get-tuple-element.36), channel_id=1, source_target_pairs={{0,24},{4,28},{8,16},{12,20},{16,8},{20,12},{24,0},{28,4},{1,25},{... | collective-permute-start | bytes 393224 | tf_op jit(solution)/shard_map/ppermute | solution.py:395
  52.4 9.3 %collective-permute-done.13.rest_5_ = f32[4,64,128]{2,1,0:T(8,128)S(1)} collective-permute-done((f32[4,64,128]{2,1,0:T(8,128)}, f32[4,64,128]{2,1,0:T(8,128)S(1)}, u32[]{:S(2)}, u32[]{:S(2)}) %collective-permute-start.13) | collective-permute-done | bytes 131104 | tf_op jit(solution)/shard_map/ppermute | solution.py:395
  61.7 5.2 %collective-permute-done.14.rest_6_ = f32[4,64,128]{2,1,0:T(8,128)S(1)} collective-permute-done((f32[4,64,128]{2,1,0:T(8,128)}, f32[4,64,128]{2,1,0:T(8,128)S(1)}, u32[]{:S(2)}, u32[]{:S(2)}) %collective-permute-start.14) | collective-permute-done | bytes 131104 | tf_op jit(solution)/shard_map/ppermute | solution.py:395
  66.9 2.8 %collective-permute-done.15.rest_7_ = f32[4,64,128]{2,1,0:T(8,128)S(1)} collective-permute-done((f32[4,64,128]{2,1,0:T(8,128)}, f32[4,64,128]{2,1,0:T(8,128)S(1)}, u32[]{:S(2)}, u32[]{:S(2)}) %collective-permute-start.15) | collective-permute-done | bytes 131104 | tf_op jit(solution)/shard_map/ppermute | solution.py:395
  69.7 2.7 %spread.1 = f32[64,4096]{1,0:T(8,128)} custom-call(s32[1]{0:T(128)} %bitcast.me_ref, s32[8,32]{1,0:T(8,128)S(1)} %bitcast.18, f32[1]{0:T(128)} %bitcast.8.power_ref, f32[64,4096]{1,0:T(8,128)S(1)} %bitcast.14, f32[4,64,128]{2,1,0:T(8,128)S(1)} %copy-done.2, f32[4,64,128]{2,1,0:T(8,128)S(1)} %collective-permute-done.9.rest_1_, ...), custom_call_target="tpu_custom_call" | custom-call | flops 524288 | bytes 3145728 | tf_op jit(solution)/shard_map/spread/pallas_call | solution.py:183
  72.4 9.1 %match.1 = f32[64,4096]{1,0:T(8,128)} custom-call(s32[1]{0:T(128)} %bitcast.me_ref, s32[8,32]{1,0:T(8,128)S(1)} %bitcast.19, bf16[352,256]{1,0:T(8,128)(2,1)S(1)} %bands.1.both_ref, f32[24,4096]{1,0:T(8,128)} %collective-permute-done.7.above_ref, f32[24,4096]{1,0:T(8,128)} %collective-permute-done.8.below_ref, f32[64,4096]{1,0:T(8,128)S(1)} %bitcast.20, ...), custom_call_target="tpu_custom_call" | custom-call | flops 4429185024 | bytes 4194304 | tf_op jit(solution)/shard_map/match/pallas_call | solution.py:342
  (35 shorter events, 2.9 us)
Async XLA Ops:
  0.6 50.5 %copy-start = (f32[16,41]{1,0:T(8,128)S(1)}, f32[16,41]{1,0:T(8,128)}, u32[]{:S(2)}) copy-start(f32[16,41]{1,0:T(8,128)} %param.16) | copy-start | bytes 7876
  3.8 6.0 %collective-permute-start = (f32[4,64,128]{2,1,0:T(8,128)}, f32[4,64,128]{2,1,0:T(8,128)S(1)}, u32[]{:S(2)}, u32[]{:S(2)}) collective-permute-start(f32[4,64,128]{2,1,0:T(8,128)} %get-tuple-element.21), channel_id=1, source_target_pairs={{0,4},{4,0},{8,12},{12,8},{16,20},{20,16},{24,28},{28,24},{1,5},{5... | collective-permute-start | bytes 393224 | tf_op jit(solution)/shard_map/ppermute | solution.py:391
  5.1 6.0 %collective-permute-start.1 = (f32[4,64,128]{2,1,0:T(8,128)}, f32[4,64,128]{2,1,0:T(8,128)S(1)}, u32[]{:S(2)}, u32[]{:S(2)}) collective-permute-start(f32[4,64,128]{2,1,0:T(8,128)} %get-tuple-element.22), channel_id=1, source_target_pairs={{0,8},{4,12},{8,0},{12,4},{16,24},{20,28},{24,16},{28,20},{1,9},{5... | collective-permute-start | bytes 393224 | tf_op jit(solution)/shard_map/ppermute | solution.py:391
  5.3 9.3 %collective-permute-start.2 = (f32[4,64,128]{2,1,0:T(8,128)}, f32[4,64,128]{2,1,0:T(8,128)S(1)}, u32[]{:S(2)}, u32[]{:S(2)}) collective-permute-start(f32[4,64,128]{2,1,0:T(8,128)} %get-tuple-element.23), channel_id=1, source_target_pairs={{0,12},{4,8},{8,4},{12,0},{16,28},{20,24},{24,20},{28,16},{1,13},{... | collective-permute-start | bytes 393224 | tf_op jit(solution)/shard_map/ppermute | solution.py:391
  6.5 9.4 %collective-permute-start.3 = (f32[4,64,128]{2,1,0:T(8,128)}, f32[4,64,128]{2,1,0:T(8,128)S(1)}, u32[]{:S(2)}, u32[]{:S(2)}) collective-permute-start(f32[4,64,128]{2,1,0:T(8,128)} %get-tuple-element.24), channel_id=1, source_target_pairs={{0,16},{4,20},{8,24},{12,28},{16,0},{20,4},{24,8},{28,12},{1,17},{... | collective-permute-start | bytes 393224 | tf_op jit(solution)/shard_map/ppermute | solution.py:391
  8.8 15.8 %collective-permute-start.4 = (f32[4,64,128]{2,1,0:T(8,128)}, f32[4,64,128]{2,1,0:T(8,128)S(1)}, u32[]{:S(2)}, u32[]{:S(2)}) collective-permute-start(f32[4,64,128]{2,1,0:T(8,128)} %get-tuple-element.25), channel_id=1, source_target_pairs={{0,20},{4,16},{8,28},{12,24},{16,4},{20,0},{24,12},{28,8},{1,21},{... | collective-permute-start | bytes 393224 | tf_op jit(solution)/shard_map/ppermute | solution.py:391
  9.9 18.5 %collective-permute-start.5 = (f32[4,64,128]{2,1,0:T(8,128)}, f32[4,64,128]{2,1,0:T(8,128)S(1)}, u32[]{:S(2)}, u32[]{:S(2)}) collective-permute-start(f32[4,64,128]{2,1,0:T(8,128)} %get-tuple-element.26), channel_id=1, source_target_pairs={{0,24},{4,28},{8,16},{12,20},{16,8},{20,12},{24,0},{28,4},{1,25},{... | collective-permute-start | bytes 393224 | tf_op jit(solution)/shard_map/ppermute | solution.py:391
  11.2 21.1 %collective-permute-start.6 = (f32[4,64,128]{2,1,0:T(8,128)}, f32[4,64,128]{2,1,0:T(8,128)S(1)}, u32[]{:S(2)}, u32[]{:S(2)}) collective-permute-start(f32[4,64,128]{2,1,0:T(8,128)} %get-tuple-element.27), channel_id=1, source_target_pairs={{0,28},{4,24},{8,20},{12,16},{16,12},{20,8},{24,4},{28,0},{1,29},{... | collective-permute-start | bytes 393224 | tf_op jit(solution)/shard_map/ppermute | solution.py:391
  11.3 21.0 %copy-start.3 = (f32[4,64,128]{2,1,0:T(8,128)S(1)}, f32[4,64,128]{2,1,0:T(8,128)}, u32[]{:S(2)}) copy-start(f32[4,64,128]{2,1,0:T(8,128)} %get-tuple-element.20.rest_0_) | copy-start | bytes 393220
  11.3 21.0 %copy-start.4 = (s32[8,32,1]{1,2,0:T(1,128)S(1)}, s32[8,32,1]{1,2,0:T(1,128)}, u32[]{:S(2)}) copy-start(s32[8,32,1]{1,2,0:T(1,128)} %param.14) | copy-start | bytes 3076
  14.6 55.1 %copy-start.1 = (f32[1,64,4096]{2,1,0:T(8,128)S(1)}, f32[1,64,4096]{2,1,0:T(8,128)}, u32[]{:S(2)}) copy-start(f32[1,64,4096]{2,1,0:T(8,128)} %param.11) | copy-start | bytes 3145732
  14.6 26.9 %collective-permute-start.9 = (f32[4,64,128]{2,1,0:T(8,128)}, f32[4,64,128]{2,1,0:T(8,128)S(1)}, u32[]{:S(2)}, u32[]{:S(2)}) collective-permute-start(f32[4,64,128]{2,1,0:T(8,128)} %get-tuple-element.31), channel_id=1, source_target_pairs={{0,4},{4,0},{8,12},{12,8},{16,20},{20,16},{24,28},{28,24},{1,5},{5... | collective-permute-start | bytes 393224 | tf_op jit(solution)/shard_map/ppermute | solution.py:395
  34.0 38.4 %collective-permute-start.7 = (f32[24,4096]{1,0:T(8,128)}, f32[24,4096]{1,0:T(8,128)}, u32[]{:S(2)}, u32[]{:S(2)}) collective-permute-start(f32[24,4096]{1,0:T(8,128)} %get-tuple-element.28), channel_id=1, source_target_pairs={{0,1},{1,2},{2,3},{4,5},{5,6},{6,7},{8,9},{9,10},{10,11},{12,13},{... | collective-permute-start | bytes 1179656 | tf_op jit(solution)/shard_map/ppermute | solution.py:405
  35.3 37.1 %collective-permute-start.8 = (f32[24,4096]{1,0:T(8,128)}, f32[24,4096]{1,0:T(8,128)}, u32[]{:S(2)}, u32[]{:S(2)}) collective-permute-start(f32[24,4096]{1,0:T(8,128)} %get-tuple-element.29), channel_id=1, source_target_pairs={{1,0},{2,1},{3,2},{5,4},{6,5},{7,6},{9,8},{10,9},{11,10},{13,12},{... | collective-permute-start | bytes 1179656 | tf_op jit(solution)/shard_map/ppermute | solution.py:406
  40.1 6.9 %collective-permute-start.10 = (f32[4,64,128]{2,1,0:T(8,128)}, f32[4,64,128]{2,1,0:T(8,128)S(1)}, u32[]{:S(2)}, u32[]{:S(2)}) collective-permute-start(f32[4,64,128]{2,1,0:T(8,128)} %get-tuple-element.32), channel_id=1, source_target_pairs={{0,8},{4,12},{8,0},{12,4},{16,24},{20,28},{24,16},{28,20},{1,9},{5... | collective-permute-start | bytes 393224 | tf_op jit(solution)/shard_map/ppermute | solution.py:395
  40.1 8.7 %collective-permute-start.11 = (f32[4,64,128]{2,1,0:T(8,128)}, f32[4,64,128]{2,1,0:T(8,128)S(1)}, u32[]{:S(2)}, u32[]{:S(2)}) collective-permute-start(f32[4,64,128]{2,1,0:T(8,128)} %get-tuple-element.33), channel_id=1, source_target_pairs={{0,12},{4,8},{8,4},{12,0},{16,28},{20,24},{24,20},{28,16},{1,13},{... | collective-permute-start | bytes 393224 | tf_op jit(solution)/shard_map/ppermute | solution.py:395
  41.5 9.6 %collective-permute-start.12 = (f32[4,64,128]{2,1,0:T(8,128)}, f32[4,64,128]{2,1,0:T(8,128)S(1)}, u32[]{:S(2)}, u32[]{:S(2)}) collective-permute-start(f32[4,64,128]{2,1,0:T(8,128)} %get-tuple-element.34), channel_id=1, source_target_pairs={{0,16},{4,20},{8,24},{12,28},{16,0},{20,4},{24,8},{28,12},{1,17},{... | collective-permute-start | bytes 393224 | tf_op jit(solution)/shard_map/ppermute | solution.py:395
  44.4 6.8 %copy-start.6 = (f32[16,41]{1,0:T(8,128)S(1)}, f32[16,41]{1,0:T(8,128)}, u32[]{:S(2)}) copy-start(f32[16,41]{1,0:T(8,128)} %param.17) | copy-start | bytes 7876
  47.0 14.7 %collective-permute-start.13 = (f32[4,64,128]{2,1,0:T(8,128)}, f32[4,64,128]{2,1,0:T(8,128)S(1)}, u32[]{:S(2)}, u32[]{:S(2)}) collective-permute-start(f32[4,64,128]{2,1,0:T(8,128)} %get-tuple-element.35), channel_id=1, source_target_pairs={{0,20},{4,16},{8,28},{12,24},{16,4},{20,0},{24,12},{28,8},{1,21},{... | collective-permute-start | bytes 393224 | tf_op jit(solution)/shard_map/ppermute | solution.py:395
  48.8 18.2 %collective-permute-start.14 = (f32[4,64,128]{2,1,0:T(8,128)}, f32[4,64,128]{2,1,0:T(8,128)S(1)}, u32[]{:S(2)}, u32[]{:S(2)}) collective-permute-start(f32[4,64,128]{2,1,0:T(8,128)} %get-tuple-element.36), channel_id=1, source_target_pairs={{0,24},{4,28},{8,16},{12,20},{16,8},{20,12},{24,0},{28,4},{1,25},{... | collective-permute-start | bytes 393224 | tf_op jit(solution)/shard_map/ppermute | solution.py:395
  51.2 18.6 %collective-permute-start.15 = (f32[4,64,128]{2,1,0:T(8,128)}, f32[4,64,128]{2,1,0:T(8,128)S(1)}, u32[]{:S(2)}, u32[]{:S(2)}) collective-permute-start(f32[4,64,128]{2,1,0:T(8,128)} %get-tuple-element.37), channel_id=1, source_target_pairs={{0,28},{4,24},{8,20},{12,16},{16,12},{20,8},{24,4},{28,0},{1,29},{... | collective-permute-start | bytes 393224 | tf_op jit(solution)/shard_map/ppermute | solution.py:395
  52.2 17.5 %copy-start.2 = (f32[4,64,128]{2,1,0:T(8,128)S(1)}, f32[4,64,128]{2,1,0:T(8,128)}, u32[]{:S(2)}) copy-start(f32[4,64,128]{2,1,0:T(8,128)} %get-tuple-element.30.rest_0_) | copy-start | bytes 393220
  69.7 2.7 %copy-start.5 = (f32[1,64,4096]{2,1,0:T(8,128)S(1)}, f32[1,64,4096]{2,1,0:T(8,128)}, u32[]{:S(2)}) copy-start(f32[1,64,4096]{2,1,0:T(8,128)} %param.10) | copy-start | bytes 3145732
where the time goes:
time: 82 us; the launch traced here: 81.5 us
  waiting for transfers between devices  34.2 us (42%)
  starting transfers between devices  21.4 us (26%)
  Pallas kernels  20.2 us (25%)
  between operations  2.69 us (3%)
  local copies, waits for them, and re-layouts  2.17 us (3%)
  matrix products  0.94 us (1%)
    ppermute x7, waiting for transfers between devices, local(): got_var[step] = lax.ppermute(mine_var[step], 'visit', pairs(step, count))  17.9 us
    ppermute x7, waiting for transfers between devices, local(): got[step] = lax.ppermute(mine[step], 'visit', pairs(step, count))  16.3 us
    pallas_call x1, Pallas kernels, match(): pl.pallas_call(functools.partial(match_kernel, margin, shifts, count, slo...  9.14 us
    ppermute x7, starting transfers between devices, local(): got_var[step] = lax.ppermute(mine_var[step], 'visit', pairs(step, count))  7.84 us
    ppermute x7, starting transfers between devices, local(): got[step] = lax.ppermute(mine[step], 'visit', pairs(step, count))  7.45 us
    pallas_call x2, Pallas kernels, cut(): pl.pallas_call(functools.partial(cut_kernel, count, slots, pieces), out_s...  6.48 us
    ppermute x1, starting transfers between devices, local(): below = lax.ppermute(head, 'tile', [(i + 1, i) for i in range(tiles - 1)])  4.81 us
    pallas_call x1, Pallas kernels, spread(): pl.pallas_call(functools.partial(spread_kernel, count, slots, pieces), ou...  2.66 us
  transfers between devices with their start and end apart: 16, of which 7 were waited for; matrix products, arithmetic and copies ran while one was open for 4% of the time, Pallas kernels for 10%

commit v1 on v0

--- a/solution.py
+++ b/solution.py
@@ -16,6 +16,7 @@
 
 SMEM = pltpu.MemorySpace.SMEM
 VMEM = pltpu.MemorySpace.VMEM
+HBM = pltpu.MemorySpace.HBM
 
 
 def partner(me, step, count):
@@ -36,13 +37,19 @@
     return [(i, (i + step) % count) for i in range(count)]
 
 
-def cut_kernel(count, slots, pieces, me_ref, owner_ref, offset_ref, strip_ref, *rest):
-    outs, (strip, cuts, starts, strip_sem, out_sems) = rest[:count], rest[count:]
-    me = me_ref[0]
+def cut_kernel(count, slots, pieces, owner_hbm, offset_hbm, strip_hbm, *rest):
+    outs, (strip, owner_ref, offset_ref, starts, sems) = rest[:count], rest[count:]
+    me = lax.axis_index("visit")
     rows, width = strip.shape
     last = width // PIECE - 1
-    load = pltpu.make_async_copy(strip_ref, strip, strip_sem)
-    load.start()
+    loads = [
+        pltpu.make_async_copy(source, target, sems.at[i])
+        for i, (source, target) in enumerate(((owner_hbm, owner_ref), (offset_hbm, offset_ref), (strip_hbm, strip)))
+    ]
+    for load in loads:
+        load.start()
+    for load in loads[:2]:
+        load.wait()
     for step in range(count):
         visit = partner(me, step, count)
         begin = step * (slots + 1)
@@ -52,9 +59,8 @@
         for k in range(pieces):
             starts[found] = offset_ref[visit, k]
             found = found + (owner_ref[visit, k] == me).astype(jnp.int32)
-    load.wait()
+    loads[2].wait()
     lane = lax.broadcasted_iota(jnp.int32, (rows, PIECE), 1)
-    stores = []
     for step in range(count):
         for slot in range(slots):
             start = starts[step * (slots + 1) + slot]
@@ -64,33 +70,27 @@
             left = strip[:, pl.ds(pl.multiple_of(block * PIECE, PIECE), PIECE)]
             right = strip[:, pl.ds(pl.multiple_of(after * PIECE, PIECE), PIECE)]
             joined = jnp.where(lane < shift, right, left)
-            cuts[step, slot] = pltpu.roll(joined, lax.rem(PIECE - shift, PIECE), 1)
-        store = pltpu.make_async_copy(cuts.at[step], outs[step], out_sems.at[step])
-        store.start()
-        stores.append(store)
-    for store in stores:
-        store.wait()
-
-
-def cut(me, owners, offsets, strip, count, slots):
-    pieces = owners.shape[1]
+            outs[step][slot] = pltpu.roll(joined, lax.rem(PIECE - shift, PIECE), 1)
+
+
+def cut(owners, offsets, strip, count, slots):
     rows, width = strip.shape
     shape = jax.ShapeDtypeStruct((slots, rows, PIECE), jnp.float32)
     return pl.pallas_call(
-        functools.partial(cut_kernel, count, slots, pieces),
+        functools.partial(cut_kernel, count, slots, owners.shape[1]),
         out_shape=[shape] * count,
-        in_specs=[pl.BlockSpec(memory_space=SMEM)] * 3 + [pl.BlockSpec(memory_space=pl.ANY)],
-        out_specs=[pl.BlockSpec(memory_space=pl.ANY)] * count,
+        in_specs=[pl.BlockSpec(memory_space=HBM)] * 3,
+        out_specs=[pl.BlockSpec(memory_space=VMEM)] * count,
         scratch_shapes=[
             pltpu.VMEM((rows, width), jnp.float32),
-            pltpu.VMEM((count, slots, rows, PIECE), jnp.float32),
+            pltpu.SMEM(owners.shape, jnp.int32),
+            pltpu.SMEM(offsets.shape, jnp.int32),
             pltpu.SMEM((count * (slots + 1),), jnp.int32),
-            pltpu.SemaphoreType.DMA,
-            pltpu.SemaphoreType.DMA((count,)),
+            pltpu.SemaphoreType.DMA((3,)),
         ],
         cost_estimate=pl.CostEstimate(flops=0, transcendentals=0, bytes_accessed=2 * strip.size * 4),
         name="cut",
-    )(me, owners, offsets, strip)
+    )(owners, offsets, strip)
 
 
 def find_places(count, slots, pieces, me, owner_ref, place, seen):
@@ -120,24 +120,26 @@
     return pl.ds(pl.multiple_of(k * PIECE, PIECE), PIECE)
 
 
-def each_slot(count, slots, me, place):
-    for step in range(count):
+def each_slot(count, slots, me, place, steps):
+    number = 0
+    for position, step in enumerate(steps):
         owner = sender(me, step, count)
         for slot in range(slots):
-            yield step, slot, place[owner * slots + slot]
+            yield number, position, slot, place[owner * slots + slot]
+            number += 1
 
 
 def places_scratch(count, slots):
     return [pltpu.SMEM((count * slots,), jnp.int32), pltpu.SMEM((count,), jnp.int32)]
 
 
-def edges_kernel(count, slots, pieces, reach, me_ref, owner_ref, *rest):
+def edges_kernel(count, slots, pieces, reach, owner_ref, *rest):
     blocks = rest[:count]
     head_ref, tail_ref, place, seen = rest[count:]
-    me = me_ref[0]
+    me = lax.axis_index("visit")
     rows = blocks[0].shape[1]
     find_places(count, slots, pieces, me, owner_ref, place, seen)
-    for position, slot, k in each_slot(count, slots, me, place):
+    for _, position, slot, k in each_slot(count, slots, me, place, range(count)):
 
         def put(position=position, slot=slot, k=k):
             head_ref[:, at_piece(k)] = blocks[position][slot, :reach]
@@ -146,50 +148,62 @@
         when_taken(count, slots, pieces, k, put)
 
 
-def edges(me, owners, blocks, width, reach):
+def edges(owners, blocks, width, reach):
     count, pieces = len(blocks), owners.shape[1]
     slots = blocks[0].shape[0]
     shape = jax.ShapeDtypeStruct((reach, width), jnp.float32)
     return pl.pallas_call(
         functools.partial(edges_kernel, count, slots, pieces, reach),
         out_shape=[shape, shape],
-        in_specs=[pl.BlockSpec(memory_space=SMEM)] * 2 + [pl.BlockSpec(memory_space=VMEM)] * count,
+        in_specs=[pl.BlockSpec(memory_space=SMEM)] + [pl.BlockSpec(memory_space=VMEM)] * count,
         out_specs=[pl.BlockSpec(memory_space=VMEM)] * 2,
         scratch_shapes=places_scratch(count, slots),
         cost_estimate=pl.CostEstimate(flops=0, transcendentals=0, bytes_accessed=4 * reach * width * 4),
         compiler_params=pltpu.CompilerParams(vmem_limit_bytes=6 << 20),
         name="edges",
-    )(me, owners, *blocks)
-
-
-def spread_kernel(count, slots, pieces, me_ref, owner_ref, power_ref, science_ref, *rest):
-    blocks = rest[:count]
-    out_ref, place, seen = rest[count:]
-    me = me_ref[0]
+    )(owners, *blocks)
+
+
+def spread_kernel(count, slots, pieces, steps, owner_ref, power_ref, science_ref, *rest):
+    blocks = rest[: len(steps)]
+    out_ref, place, seen, held, sems = rest[-5:]
+    me = lax.axis_index("visit")
     power = power_ref[0]
     find_places(count, slots, pieces, me, owner_ref, place, seen)
-    for position, slot, k in each_slot(count, slots, me, place):
-
-        def put(position=position, slot=slot, k=k):
-            out_ref[:, at_piece(k)] = science_ref[:, at_piece(k)] + power * blocks[position][slot]
-
-        when_taken(count, slots, pieces, k, put)
-
-
-def spread(me, owners, power, science_var, blocks):
-    count, pieces = len(blocks), owners.shape[1]
-    slots = blocks[0].shape[0]
-    size = science_var.size
+    for stage in range(2):
+        for number, position, slot, k in each_slot(count, slots, me, place, steps):
+
+            def go(number=number, position=position, slot=slot, k=k, stage=stage):
+                store = pltpu.make_async_copy(held.at[number], out_ref.at[:, at_piece(k)], sems.at[number])
+                if stage == 0:
+                    held[number] = science_ref[:, at_piece(k)] + power * blocks[position][slot]
+                    store.start()
+                else:
+                    store.wait()
+
+            when_taken(count, slots, pieces, k, go)
+
+
+def spread(owners, power, science_var, blocks, steps, count, partial=None):
+    pieces = owners.shape[1]
+    slots, rows = blocks[0].shape[:2]
+    number = slots * len(steps)
+    size = number * rows * PIECE
+    before = [] if partial is None else [partial]
     return pl.pallas_call(
-        functools.partial(spread_kernel, count, slots, pieces),
+        functools.partial(spread_kernel, count, slots, pieces, steps),
         out_shape=jax.ShapeDtypeStruct(science_var.shape, jnp.float32),
-        in_specs=[pl.BlockSpec(memory_space=SMEM)] * 3 + [pl.BlockSpec(memory_space=VMEM)] * (1 + count),
-        out_specs=pl.BlockSpec(memory_space=VMEM),
-        scratch_shapes=places_scratch(count, slots),
+        in_specs=[pl.BlockSpec(memory_space=SMEM)] * 2
+        + [pl.BlockSpec(memory_space=VMEM)] * (1 + len(steps))
+        + [pl.BlockSpec(memory_space=pl.ANY)] * len(before),
+        out_specs=pl.BlockSpec(memory_space=pl.ANY),
+        input_output_aliases={3 + len(steps): 0} if before else {},
+        scratch_shapes=places_scratch(count, slots)
+        + [pltpu.VMEM((number, rows, PIECE), jnp.float32), pltpu.SemaphoreType.DMA((number,))],
         cost_estimate=pl.CostEstimate(flops=2 * size, transcendentals=0, bytes_accessed=3 * size * 4),
         compiler_params=pltpu.CompilerParams(vmem_limit_bytes=6 << 20),
         name="spread",
-    )(me, owners, power, science_var, *blocks)
+    )(owners, power, science_var, *blocks, *before)
 
 
 def split(x):
@@ -230,18 +244,18 @@
     return pltpu.roll(x, PIECE - lanes, 1)
 
 
-def match_kernel(margin, shifts, count, slots, pieces, me_ref, owner_ref, both_ref, above_ref, below_ref, science_ref, *rest):
+def match_kernel(margin, shifts, count, slots, pieces, owner_ref, both_ref, above_ref, below_ref, science_ref, *rest):
     images, out_ref, rest = rest[:count], rest[count], rest[count + 1 :]
-    place, seen, wide, high0, high1, low0, low1, part0, part1, kept_image, kept_part = rest
+    place, seen, wide, high0, high1, low0, low1, part0, part1, kept_image, kept_part, result, sems = rest
     rows, width = science_ref.shape
     reach = above_ref.shape[0]
     window = SUB + 2 * reach
     filled = rows + 2 * reach
     half = both_ref.shape[0] // 2
     high, low, part = (high0, high1), (low0, low1), (part0, part1)
-    me = me_ref[0]
+    me = lax.axis_index("visit")
     find_places(count, slots, pieces, me, owner_ref, place, seen)
-    for position, slot, k in each_slot(count, slots, me, place):
+    for _, position, slot, k in each_slot(count, slots, me, place, range(count)):
 
         def put(position=position, slot=slot, k=k):
             wide[reach : reach + rows, at_piece(k + 1)] = images[position][slot]
@@ -254,6 +268,10 @@
     blocks = width // BLOCK
     lane_image = lax.broadcasted_iota(jnp.int32, (filled, PIECE), 1)
     lane_part = lax.broadcasted_iota(jnp.int32, (SUB, PIECE), 1)
+
+    def store(b):
+        columns = pl.ds(pl.multiple_of(b * BLOCK, BLOCK), BLOCK)
+        return pltpu.make_async_copy(result.at[:, columns], out_ref.at[:, columns], sems.at[b])
 
     def build(b, parity, first=False):
         begin = b * BLOCK
@@ -309,7 +327,8 @@
                     totals[k] = totals[k] + jnp.where(lane_part < PIECE - q, turned[k], turned[k + 1])
             for k in (0, 1):
                 at = pl.ds(pl.multiple_of(begin + k * PIECE, PIECE), PIECE)
-                out_ref[top : top + SUB, at] = science_ref[top : top + SUB, at] - totals[k]
+                result[top : top + SUB, at] = science_ref[top : top + SUB, at] - totals[k]
+        store(b).start()
 
     build(0, 0, first=True)
     build(1, 1)
@@ -331,9 +350,11 @@
     join(blocks - 2, 0)
     multiply(0, PIECE)
     join(blocks - 1, 1)
-
-
-def match(margin, shifts, me, owners, both, above, below, science, images):
+    for b in range(blocks):
+        store(b).wait()
+
+
+def match(margin, shifts, owners, both, above, below, science, images):
     rows, width = science.shape
     count, pieces = len(images), owners.shape[1]
     slots = images[0].shape[0]
@@ -342,9 +363,9 @@
     return pl.pallas_call(
         functools.partial(match_kernel, margin, shifts, count, slots, pieces),
         out_shape=jax.ShapeDtypeStruct(science.shape, jnp.float32),
-        in_specs=[pl.BlockSpec(memory_space=SMEM)] * 2
+        in_specs=[pl.BlockSpec(memory_space=SMEM)]
         + [pl.BlockSpec(memory_space=VMEM)] * (4 + count),
-        out_specs=pl.BlockSpec(memory_space=VMEM),
+        out_specs=pl.BlockSpec(memory_space=pl.ANY),
         scratch_shapes=places_scratch(count, slots)
         + [
             pltpu.VMEM((filled, width + BLOCK + 2 * PIECE), jnp.float32),
@@ -352,13 +373,15 @@
             *[pltpu.VMEM((GROUP * rows, BLOCK), jnp.float32)] * 2,
             pltpu.VMEM((shifts * filled, PIECE), jnp.float32),
             pltpu.VMEM((GROUP * rows, PIECE), jnp.float32),
+            pltpu.VMEM((rows, width), jnp.float32),
+            pltpu.SemaphoreType.DMA((width // BLOCK,)),
         ],
         cost_estimate=pl.CostEstimate(
             flops=6 * GROUP * rows * both.shape[1] * width, transcendentals=0, bytes_accessed=4 * rows * width * 4
         ),
         compiler_params=pltpu.CompilerParams(vmem_limit_bytes=20 << 20),
         name="match",
-    )(me, owners, both, above, below, science, *images)
+    )(owners, both, above, below, science, *images)
 
 
 def local(
@@ -383,15 +406,14 @@
     me = lax.axis_index("visit")
     tile_me = lax.axis_index("tile")
     highest = lax.Precision.HIGHEST
-    me_ref = me.astype(jnp.int32).reshape(1)
     owners = intersection[:, :, 0]
-    mine = cut(me_ref, owners, col_offset, template[0], count, slots)
-    got = [mine[0]] + [None] * (count - 1)
-    for step in steps(count):
+    mine = cut(owners, col_offset, template[0], count, slots)
+    got = list(mine)
+    for step in flux_steps(count):
         got[step] = lax.ppermute(mine[step], "visit", pairs(step, count))
-    mine_var = cut(me_ref, owners, col_offset, template_var[0], count, slots)
-    got_var = [mine_var[0]] + [None] * (count - 1)
-    for step in steps(count):
+    mine_var = cut(owners, col_offset, template_var[0], count, slots)
+    got_var = list(mine_var)
+    for step in near_steps(count) + far_steps(count):
         got_var[step] = lax.ppermute(mine_var[step], "visit", pairs(step, count))
 
     chosen = lax.dynamic_slice(tile_coef, (me, tile_me), (1, 1))[0, 0]
@@ -400,18 +422,32 @@
     power = jnp.sum(taps * taps).reshape(1)
     both = bands(taps, SUB + 2 * reach, reach - margin)
 
-    head, tail = edges(me_ref, owners, got, width, reach)
+    head, tail = edges(owners, got, width, reach)
     tiles = lax.axis_size("tile")
     above = lax.ppermute(tail, "tile", [(i, i + 1) for i in range(tiles - 1)])
     below = lax.ppermute(head, "tile", [(i + 1, i) for i in range(tiles - 1)])
+    first = [0] + near_steps(count)
+    blocks = [got_var[step] for step in first]
+    difference_var = spread(owners, power, science_var[0], blocks, first, count)
     shifts = -(-side // GROUP)
-    difference = match(margin, shifts, me_ref, owners, both, above, below, science[0], got)
-    difference_var = spread(me_ref, owners, power, science_var[0], got_var)
+    difference = match(margin, shifts, owners, both, above, below, science[0], got)
+    second = far_steps(count)
+    blocks = [got_var[step] for step in second]
+    difference_var = spread(owners, power, science_var[0], blocks, second, count, difference_var)
     return difference[None], difference_var[None]
 
 
-def steps(count):
-    return sorted(range(1, count), key=lambda step: -(step.bit_length()))
+def near_steps(count):
+    return list(range(1, count // 2))
+
+
+def far_steps(count):
+    return list(range(count // 2, count))
+
+
+def flux_steps(count):
+    far = far_steps(count)
+    return far[-1:] + near_steps(count) + far[1:-1] + far[:1]
 
 
 def solution(mesh):

time: 82 us -> 82.7 us (level)
  the two profiles are of different devices: /device:TPU:11 before, /device:TPU:18 now
where the time goes in v1:
time: 82.7 us; the launch traced here: 82.4 us
  waiting for transfers between devices  32.4 us (39%)
  starting transfers between devices  22.3 us (27%)
  Pallas kernels  21.2 us (26%)
  local copies, waits for them, and re-layouts  2.85 us (3%)
  between operations  2.75 us (3%)
  matrix products  0.93 us (1%)
    ppermute x7, waiting for transfers between devices, local(): got[step] = lax.ppermute(mine[step], 'visit', pairs(step, count))  20 us
    ppermute x7, waiting for transfers between devices, local(): got_var[step] = lax.ppermute(mine_var[step], 'visit', pairs(step, count))  12.4 us
    pallas_call x1, Pallas kernels, match(): pl.pallas_call(functools.partial(match_kernel, margin, shifts, count, slo...  8.95 us
    ppermute x7, starting transfers between devices, local(): got_var[step] = lax.ppermute(mine_var[step], 'visit', pairs(step, count))  8.85 us
    ppermute x7, starting transfers between devices, local(): got[step] = lax.ppermute(mine[step], 'visit', pairs(step, count))  7.89 us
    pallas_call x2, Pallas kernels, cut(): pl.pallas_call(functools.partial(cut_kernel, count, slots, owners.shape[1...  5.68 us
    pallas_call x2, Pallas kernels, spread(): pl.pallas_call(functools.partial(spread_kernel, count, slots, pieces, ste...  4.66 us
    ppermute x1, starting transfers between devices, local(): below = lax.ppermute(head, 'tile', [(i + 1, i) for i in range(tiles - 1)])  3.64 us
  transfers between devices with their start and end apart: 16, of which 8 were waited for; matrix products, arithmetic and copies ran while one was open for 4% of the time, Pallas kernels for 11%

profile of v1, /device:TPU:18, one launch (start us, length us, event | category | flops | bytes accessed | tf_op | source)
XLA Modules:
  0.0 82.4 jit_solution(3368396018898293230)
XLA Ops:
  0.6 2.8 %cut.2 = (f32[4,64,128]{2,1,0:T(8,128)}, f32[4,64,128]{2,1,0:T(8,128)}, f32[4,64,128]{2,1,0:T(8,128)}, f32[4,64,128]{2,1,0:T(8,128)}, f32[4,64,128]{2,1,0:T(8,12...) custom-call(s32[8,32]{1,0:T(8,128)} %bitcast.15, s32[8,32]{1,0:T(8,128)} %offset_hbm.3, ...), custom_call_target="tpu_custom_call" | custom-call | bytes 2097152 | tf_op jit(solution)/shard_map/cut/pallas_call | solution.py:79
  3.4 1.6 %collective-permute-start = (f32[4,64,128]{2,1,0:T(8,128)}, f32[4,64,128]{2,1,0:T(8,128)S(1)}, u32[]{:S(2)}, u32[]{:S(2)}) collective-permute-start(f32[4,64,128]{2,1,0:T(8,128)} %get-tuple-element.21), channel_id=1, source_target_pairs={{0,4},{4,0},{8,12},{12,8},{16,20},{20,16},{24,28},{28,24},{1,5},{5... | collective-permute-start | bytes 393224 | tf_op jit(solution)/shard_map/ppermute | solution.py:413
  5.0 1.6 %collective-permute-start.1 = (f32[4,64,128]{2,1,0:T(8,128)}, f32[4,64,128]{2,1,0:T(8,128)S(1)}, u32[]{:S(2)}, u32[]{:S(2)}) collective-permute-start(f32[4,64,128]{2,1,0:T(8,128)} %get-tuple-element.22), channel_id=1, source_target_pairs={{0,8},{4,12},{8,0},{12,4},{16,24},{20,28},{24,16},{28,20},{1,9},{5... | collective-permute-start | bytes 393224 | tf_op jit(solution)/shard_map/ppermute | solution.py:413
  7.3 3.5 %collective-permute-start.4 = (f32[4,64,128]{2,1,0:T(8,128)}, f32[4,64,128]{2,1,0:T(8,128)S(1)}, u32[]{:S(2)}, u32[]{:S(2)}) collective-permute-start(f32[4,64,128]{2,1,0:T(8,128)} %get-tuple-element.25), channel_id=1, source_target_pairs={{0,20},{4,16},{8,28},{12,24},{16,4},{20,0},{24,12},{28,8},{1,21},{... | collective-permute-start | bytes 393224 | tf_op jit(solution)/shard_map/ppermute | solution.py:413
  11.3 2.6 %collective-permute-done.1.rest_2_ = f32[4,64,128]{2,1,0:T(8,128)S(1)} collective-permute-done((f32[4,64,128]{2,1,0:T(8,128)}, f32[4,64,128]{2,1,0:T(8,128)S(1)}, u32[]{:S(2)}, u32[]{:S(2)}) %collective-permute-start.1) | collective-permute-done | bytes 131104 | tf_op jit(solution)/shard_map/ppermute | solution.py:413
  13.9 2.9 %cut.3 = (f32[4,64,128]{2,1,0:T(8,128)}, f32[4,64,128]{2,1,0:T(8,128)}, f32[4,64,128]{2,1,0:T(8,128)}, f32[4,64,128]{2,1,0:T(8,128)}, f32[4,64,128]{2,1,0:T(8,12...) custom-call(s32[8,32]{1,0:T(8,128)} %bitcast.16, s32[8,32]{1,0:T(8,128)} %offset_hbm.3, ...), custom_call_target="tpu_custom_call" | custom-call | bytes 2097152 | tf_op jit(solution)/shard_map/cut/pallas_call | solution.py:79
  16.9 3.1 %collective-permute-start.9 = (f32[4,64,128]{2,1,0:T(8,128)}, f32[4,64,128]{2,1,0:T(8,128)S(1)}, u32[]{:S(2)}, u32[]{:S(2)}) collective-permute-start(f32[4,64,128]{2,1,0:T(8,128)} %get-tuple-element.30), channel_id=1, source_target_pairs={{0,16},{4,20},{8,24},{12,28},{16,0},{20,4},{24,8},{28,12},{1,17},{... | collective-permute-start | bytes 393224 | tf_op jit(solution)/shard_map/ppermute | solution.py:417
  20.0 8.3 %collective-permute-done.4.rest_5_ = f32[4,64,128]{2,1,0:T(8,128)S(1)} collective-permute-done((f32[4,64,128]{2,1,0:T(8,128)}, f32[4,64,128]{2,1,0:T(8,128)S(1)}, u32[]{:S(2)}, u32[]{:S(2)}) %collective-permute-start.4) | collective-permute-done | bytes 131104 | tf_op jit(solution)/shard_map/ppermute | solution.py:413
  28.3 5.8 %collective-permute-done.5.rest_6_ = f32[4,64,128]{2,1,0:T(8,128)S(1)} collective-permute-done((f32[4,64,128]{2,1,0:T(8,128)}, f32[4,64,128]{2,1,0:T(8,128)S(1)}, u32[]{:S(2)}, u32[]{:S(2)}) %collective-permute-start.5) | collective-permute-done | bytes 131104 | tf_op jit(solution)/shard_map/ppermute | solution.py:413
  34.1 3.3 %collective-permute-done.6.rest_7_ = f32[4,64,128]{2,1,0:T(8,128)S(1)} collective-permute-done((f32[4,64,128]{2,1,0:T(8,128)}, f32[4,64,128]{2,1,0:T(8,128)S(1)}, u32[]{:S(2)}, u32[]{:S(2)}) %collective-permute-start.6) | collective-permute-done | bytes 131104 | tf_op jit(solution)/shard_map/ppermute | solution.py:413
  37.3 1.8 %edges.1 = (f32[24,4096]{1,0:T(8,128)}, f32[24,4096]{1,0:T(8,128)}) custom-call(s32[8,32]{1,0:T(8,128)S(1)} %bitcast.17, f32[4,64,128]{2,1,0:T(8,128)S(1)} %copy-done.3, f32[4,64,128]{2,1,0:T(8,128)S(1)} %collective-permute-done.rest_1_, f32[4,64,128]{2,1,0:T(8,128)S(1)} %collective-permute-done.1.rest_2_, f32[4,64,128]{2,1,0:T(8,128)S(1)} %collective-permute-done.2.rest_3_, ...), custom_call_target="tpu_custom_call" | custom-call | bytes 1572864 | tf_op jit(solution)/shard_map/edges/pallas_call | solution.py:155
  39.1 1.9 %collective-permute-start.7 = (f32[24,4096]{1,0:T(8,128)}, f32[24,4096]{1,0:T(8,128)}, u32[]{:S(2)}, u32[]{:S(2)}) collective-permute-start(f32[24,4096]{1,0:T(8,128)} %get-tuple-element.28), channel_id=1, source_target_pairs={{0,1},{1,2},{2,3},{4,5},{5,6},{6,7},{8,9},{9,10},{10,11},{12,13},{... | collective-permute-start | bytes 1179656 | tf_op jit(solution)/shard_map/ppermute | solution.py:427
  41.0 3.6 %collective-permute-start.8 = (f32[24,4096]{1,0:T(8,128)}, f32[24,4096]{1,0:T(8,128)}, u32[]{:S(2)}, u32[]{:S(2)}) collective-permute-start(f32[24,4096]{1,0:T(8,128)} %get-tuple-element.29), channel_id=1, source_target_pairs={{1,0},{2,1},{3,2},{5,4},{6,5},{7,6},{9,8},{10,9},{11,10},{13,12},{... | collective-permute-start | bytes 1179656 | tf_op jit(solution)/shard_map/ppermute | solution.py:428
  44.6 0.7 collective-permute-start.13
  45.4 2.8 %collective-permute-start.15 = (f32[4,64,128]{2,1,0:T(8,128)}, f32[4,64,128]{2,1,0:T(8,128)S(1)}, u32[]{:S(2)}, u32[]{:S(2)}) collective-permute-start(f32[4,64,128]{2,1,0:T(8,128)} %get-tuple-element.37), channel_id=1, source_target_pairs={{0,12},{4,8},{8,4},{12,0},{16,28},{20,24},{24,20},{28,16},{1,13},{... | collective-permute-start | bytes 393224 | tf_op jit(solution)/shard_map/ppermute | solution.py:417
  48.2 1.3 %dynamic_slice.7 = s32[1,1]{0,1:T(1,128)} dynamic-slice(s32[8,4]{0,1:T(4,128)} %param.19, s32[]{:T(128)S(6)} %select_n.10, s32[]{:T(128)S(6)} %select_n.11), dynamic_slice_sizes={1,1} | dynamic-slice | bytes 12 | tf_op jit(solution)/shard_map/dynamic_slice | solution.py:419
  52.1 1.5 %collective-permute-start.11 = (f32[4,64,128]{2,1,0:T(8,128)}, f32[4,64,128]{2,1,0:T(8,128)S(1)}, u32[]{:S(2)}, u32[]{:S(2)}) collective-permute-start(f32[4,64,128]{2,1,0:T(8,128)} %get-tuple-element.32), channel_id=1, source_target_pairs={{0,24},{4,28},{8,16},{12,20},{16,8},{20,12},{24,0},{28,4},{1,25},{... | collective-permute-start | bytes 393224 | tf_op jit(solution)/shard_map/ppermute | solution.py:417
  54.6 0.9 %multiply_reduce_fusion = (f32[]{:T(128)}, f32[41,41]{1,0:T(8,128)S(1)}) fusion(f32[16,41]{1,0:T(8,128)S(1)} %copy-done, f32[16,41]{1,0:T(8,128)S(1)} %copy-done.6, f32[16]{0:T(128)S(1)} %dynamic-slice_bitcast_fusion), kind=kOutput, calls=%fused_computation | convolution fusion | flops 326769 | bytes 12040 | tf_op jit(solution)/shard_map/bc,ba->ca/dot_general | solution.py:421
  56.5 2.3 %spread.2.rest_4_ = f32[64,4096]{1,0:T(8,128)} custom-call(s32[8,32]{1,0:T(8,128)S(1)} %bitcast.18, f32[1]{0:T(128)} %bitcast.7.power_ref, f32[64,4096]{1,0:T(8,128)S(1)} %bitcast.13, f32[4,64,128]{2,1,0:T(8,128)S(1)} %copy-done.2, f32[4,64,128]{2,1,0:T(8,128)S(1)} %collective-permute-done.13.rest_1_, f32[4,64,128]{2,1,0:T(8,128)S(1)} %collective-permute-done.14.rest_2_, ...), custom_call_target="tpu_custom_call" | custom-call | flops 262144 | bytes 1572864 | tf_op jit(solution)/shard_map/spread/pallas_call | solution.py:193
  58.9 4.5 %collective-permute-done.10.rest_1_ = f32[4,64,128]{2,1,0:T(8,128)S(1)} collective-permute-done((f32[4,64,128]{2,1,0:T(8,128)}, f32[4,64,128]{2,1,0:T(8,128)S(1)}, u32[]{:S(2)}, u32[]{:S(2)}) %collective-permute-start.10) | collective-permute-done | bytes 131104 | tf_op jit(solution)/shard_map/ppermute | solution.py:417
  63.4 5.3 %collective-permute-done.11.rest_2_ = f32[4,64,128]{2,1,0:T(8,128)S(1)} collective-permute-done((f32[4,64,128]{2,1,0:T(8,128)}, f32[4,64,128]{2,1,0:T(8,128)S(1)}, u32[]{:S(2)}, u32[]{:S(2)}) %collective-permute-start.11) | collective-permute-done | bytes 131104 | tf_op jit(solution)/shard_map/ppermute | solution.py:417
  68.7 2.4 %collective-permute-done.12.rest_3_ = f32[4,64,128]{2,1,0:T(8,128)S(1)} collective-permute-done((f32[4,64,128]{2,1,0:T(8,128)}, f32[4,64,128]{2,1,0:T(8,128)S(1)}, u32[]{:S(2)}, u32[]{:S(2)}) %collective-permute-start.12) | collective-permute-done | bytes 131104 | tf_op jit(solution)/shard_map/ppermute | solution.py:417
  71.0 2.3 %spread.3 = f32[64,4096]{1,0:T(8,128)} custom-call(s32[8,32]{1,0:T(8,128)S(1)} %bitcast.19, f32[1]{0:T(128)} %bitcast.7.power_ref, f32[64,4096]{1,0:T(8,128)S(1)} %bitcast.14, f32[4,64,128]{2,1,0:T(8,128)S(1)} %collective-permute-done.9.rest_0_, f32[4,64,128]{2,1,0:T(8,128)S(1)} %collective-permute-done.10.rest_1_, ...), custom_call_target="tpu_custom_call", output_to_operand_aliasing={{}: (7, {})} | custom-call | flops 262144 | bytes 1572864 | tf_op jit(solution)/shard_map/spread/pallas_call | solution.py:193
  73.4 8.9 %match.1 = f32[64,4096]{1,0:T(8,128)} custom-call(s32[8,32]{1,0:T(8,128)S(1)} %bitcast.20, bf16[352,256]{1,0:T(8,128)(2,1)S(1)} %bands.1.both_ref, f32[24,4096]{1,0:T(8,128)} %collective-permute-done.7.above_ref, f32[24,4096]{1,0:T(8,128)} %collective-permute-done.8.below_ref, f32[64,4096]{1,0:T(8,128)S(1)} %bitcast.21, f32[4,64,128]{2,1,0:T(8,128)S(1)} %copy-done.3, ...), custom_call_target="tpu_custom_call" | custom-call | flops 4429185024 | bytes 4194304 | tf_op jit(solution)/shard_map/match/pallas_call | solution.py:363
  (36 shorter events, 3.8 us)
Async XLA Ops:
  0.6 53.9 %copy-start = (f32[16,41]{1,0:T(8,128)S(1)}, f32[16,41]{1,0:T(8,128)}, u32[]{:S(2)}) copy-start(f32[16,41]{1,0:T(8,128)} %param.16) | copy-start | bytes 7876
  3.4 7.4 %collective-permute-start = (f32[4,64,128]{2,1,0:T(8,128)}, f32[4,64,128]{2,1,0:T(8,128)S(1)}, u32[]{:S(2)}, u32[]{:S(2)}) collective-permute-start(f32[4,64,128]{2,1,0:T(8,128)} %get-tuple-element.21), channel_id=1, source_target_pairs={{0,4},{4,0},{8,12},{12,8},{16,20},{20,16},{24,28},{28,24},{1,5},{5... | collective-permute-start | bytes 393224 | tf_op jit(solution)/shard_map/ppermute | solution.py:413
  5.0 8.9 %collective-permute-start.1 = (f32[4,64,128]{2,1,0:T(8,128)}, f32[4,64,128]{2,1,0:T(8,128)S(1)}, u32[]{:S(2)}, u32[]{:S(2)}) collective-permute-start(f32[4,64,128]{2,1,0:T(8,128)} %get-tuple-element.22), channel_id=1, source_target_pairs={{0,8},{4,12},{8,0},{12,4},{16,24},{20,28},{24,16},{28,20},{1,9},{5... | collective-permute-start | bytes 393224 | tf_op jit(solution)/shard_map/ppermute | solution.py:413
  6.6 10.3 %collective-permute-start.2 = (f32[4,64,128]{2,1,0:T(8,128)}, f32[4,64,128]{2,1,0:T(8,128)S(1)}, u32[]{:S(2)}, u32[]{:S(2)}) collective-permute-start(f32[4,64,128]{2,1,0:T(8,128)} %get-tuple-element.23), channel_id=1, source_target_pairs={{0,12},{4,8},{8,4},{12,0},{16,28},{20,24},{24,20},{28,16},{1,13},{... | collective-permute-start | bytes 393224 | tf_op jit(solution)/shard_map/ppermute | solution.py:413
  7.0 13.1 %collective-permute-start.3 = (f32[4,64,128]{2,1,0:T(8,128)}, f32[4,64,128]{2,1,0:T(8,128)S(1)}, u32[]{:S(2)}, u32[]{:S(2)}) collective-permute-start(f32[4,64,128]{2,1,0:T(8,128)} %get-tuple-element.24), channel_id=1, source_target_pairs={{0,16},{4,20},{8,24},{12,28},{16,0},{20,4},{24,8},{28,12},{1,17},{... | collective-permute-start | bytes 393224 | tf_op jit(solution)/shard_map/ppermute | solution.py:413
  7.3 21.0 %collective-permute-start.4 = (f32[4,64,128]{2,1,0:T(8,128)}, f32[4,64,128]{2,1,0:T(8,128)S(1)}, u32[]{:S(2)}, u32[]{:S(2)}) collective-permute-start(f32[4,64,128]{2,1,0:T(8,128)} %get-tuple-element.25), channel_id=1, source_target_pairs={{0,20},{4,16},{8,28},{12,24},{16,4},{20,0},{24,12},{28,8},{1,21},{... | collective-permute-start | bytes 393224 | tf_op jit(solution)/shard_map/ppermute | solution.py:413
  10.8 23.2 %collective-permute-start.5 = (f32[4,64,128]{2,1,0:T(8,128)}, f32[4,64,128]{2,1,0:T(8,128)S(1)}, u32[]{:S(2)}, u32[]{:S(2)}) collective-permute-start(f32[4,64,128]{2,1,0:T(8,128)} %get-tuple-element.26), channel_id=1, source_target_pairs={{0,24},{4,28},{8,16},{12,20},{16,8},{20,12},{24,0},{28,4},{1,25},{... | collective-permute-start | bytes 393224 | tf_op jit(solution)/shard_map/ppermute | solution.py:413
  13.9 23.4 %collective-permute-start.6 = (f32[4,64,128]{2,1,0:T(8,128)}, f32[4,64,128]{2,1,0:T(8,128)S(1)}, u32[]{:S(2)}, u32[]{:S(2)}) collective-permute-start(f32[4,64,128]{2,1,0:T(8,128)} %get-tuple-element.27), channel_id=1, source_target_pairs={{0,28},{4,24},{8,20},{12,16},{16,12},{20,8},{24,4},{28,0},{1,29},{... | collective-permute-start | bytes 393224 | tf_op jit(solution)/shard_map/ppermute | solution.py:413
  13.9 23.4 %copy-start.3 = (f32[4,64,128]{2,1,0:T(8,128)S(1)}, f32[4,64,128]{2,1,0:T(8,128)}, u32[]{:S(2)}) copy-start(f32[4,64,128]{2,1,0:T(8,128)} %get-tuple-element.20.rest_0_) | copy-start | bytes 393220
  13.9 23.4 %copy-start.4 = (s32[8,32,1]{1,2,0:T(1,128)S(1)}, s32[8,32,1]{1,2,0:T(1,128)}, u32[]{:S(2)}) copy-start(s32[8,32,1]{1,2,0:T(1,128)} %param.14) | copy-start | bytes 3076
  16.9 39.0 %copy-start.1 = (f32[1,64,4096]{2,1,0:T(8,128)S(1)}, f32[1,64,4096]{2,1,0:T(8,128)}, u32[]{:S(2)}) copy-start(f32[1,64,4096]{2,1,0:T(8,128)} %param.11) | copy-start | bytes 3145732
  16.9 28.5 %collective-permute-start.9 = (f32[4,64,128]{2,1,0:T(8,128)}, f32[4,64,128]{2,1,0:T(8,128)S(1)}, u32[]{:S(2)}, u32[]{:S(2)}) collective-permute-start(f32[4,64,128]{2,1,0:T(8,128)} %get-tuple-element.30), channel_id=1, source_target_pairs={{0,16},{4,20},{8,24},{12,28},{16,0},{20,4},{24,8},{28,12},{1,17},{... | collective-permute-start | bytes 393224 | tf_op jit(solution)/shard_map/ppermute | solution.py:417
  39.1 34.3 %collective-permute-start.7 = (f32[24,4096]{1,0:T(8,128)}, f32[24,4096]{1,0:T(8,128)}, u32[]{:S(2)}, u32[]{:S(2)}) collective-permute-start(f32[24,4096]{1,0:T(8,128)} %get-tuple-element.28), channel_id=1, source_target_pairs={{0,1},{1,2},{2,3},{4,5},{5,6},{6,7},{8,9},{9,10},{10,11},{12,13},{... | collective-permute-start | bytes 1179656 | tf_op jit(solution)/shard_map/ppermute | solution.py:427
  41.0 32.4 %collective-permute-start.8 = (f32[24,4096]{1,0:T(8,128)}, f32[24,4096]{1,0:T(8,128)}, u32[]{:S(2)}, u32[]{:S(2)}) collective-permute-start(f32[24,4096]{1,0:T(8,128)} %get-tuple-element.29), channel_id=1, source_target_pairs={{1,0},{2,1},{3,2},{5,4},{6,5},{7,6},{9,8},{10,9},{11,10},{13,12},{... | collective-permute-start | bytes 1179656 | tf_op jit(solution)/shard_map/ppermute | solution.py:428
  44.6 7.5 %collective-permute-start.13 = (f32[4,64,128]{2,1,0:T(8,128)}, f32[4,64,128]{2,1,0:T(8,128)S(1)}, u32[]{:S(2)}, u32[]{:S(2)}) collective-permute-start(f32[4,64,128]{2,1,0:T(8,128)} %get-tuple-element.35), channel_id=1, source_target_pairs={{0,4},{4,0},{8,12},{12,8},{16,20},{20,16},{24,28},{28,24},{1,5},{5... | collective-permute-start | bytes 393224 | tf_op jit(solution)/shard_map/ppermute | solution.py:417
  45.4 6.8 %collective-permute-start.14 = (f32[4,64,128]{2,1,0:T(8,128)}, f32[4,64,128]{2,1,0:T(8,128)S(1)}, u32[]{:S(2)}, u32[]{:S(2)}) collective-permute-start(f32[4,64,128]{2,1,0:T(8,128)} %get-tuple-element.36), channel_id=1, source_target_pairs={{0,8},{4,12},{8,0},{12,4},{16,24},{20,28},{24,16},{28,20},{1,9},{5... | collective-permute-start | bytes 393224 | tf_op jit(solution)/shard_map/ppermute | solution.py:417
  45.4 8.6 %collective-permute-start.15 = (f32[4,64,128]{2,1,0:T(8,128)}, f32[4,64,128]{2,1,0:T(8,128)S(1)}, u32[]{:S(2)}, u32[]{:S(2)}) collective-permute-start(f32[4,64,128]{2,1,0:T(8,128)} %get-tuple-element.37), channel_id=1, source_target_pairs={{0,12},{4,8},{8,4},{12,0},{16,28},{20,24},{24,20},{28,16},{1,13},{... | collective-permute-start | bytes 393224 | tf_op jit(solution)/shard_map/ppermute | solution.py:417
  49.5 5.1 %copy-start.6 = (f32[16,41]{1,0:T(8,128)S(1)}, f32[16,41]{1,0:T(8,128)}, u32[]{:S(2)}) copy-start(f32[16,41]{1,0:T(8,128)} %param.17) | copy-start | bytes 7876
  52.1 11.3 %collective-permute-start.10 = (f32[4,64,128]{2,1,0:T(8,128)}, f32[4,64,128]{2,1,0:T(8,128)S(1)}, u32[]{:S(2)}, u32[]{:S(2)}) collective-permute-start(f32[4,64,128]{2,1,0:T(8,128)} %get-tuple-element.31), channel_id=1, source_target_pairs={{0,20},{4,16},{8,28},{12,24},{16,4},{20,0},{24,12},{28,8},{1,21},{... | collective-permute-start | bytes 393224 | tf_op jit(solution)/shard_map/ppermute | solution.py:417
  52.1 16.5 %collective-permute-start.11 = (f32[4,64,128]{2,1,0:T(8,128)}, f32[4,64,128]{2,1,0:T(8,128)S(1)}, u32[]{:S(2)}, u32[]{:S(2)}) collective-permute-start(f32[4,64,128]{2,1,0:T(8,128)} %get-tuple-element.32), channel_id=1, source_target_pairs={{0,24},{4,28},{8,16},{12,20},{16,8},{20,12},{24,0},{28,4},{1,25},{... | collective-permute-start | bytes 393224 | tf_op jit(solution)/shard_map/ppermute | solution.py:417
  53.9 17.1 %collective-permute-start.12 = (f32[4,64,128]{2,1,0:T(8,128)}, f32[4,64,128]{2,1,0:T(8,128)S(1)}, u32[]{:S(2)}, u32[]{:S(2)}) collective-permute-start(f32[4,64,128]{2,1,0:T(8,128)} %get-tuple-element.33), channel_id=1, source_target_pairs={{0,28},{4,24},{8,20},{12,16},{16,12},{20,8},{24,4},{28,0},{1,29},{... | collective-permute-start | bytes 393224 | tf_op jit(solution)/shard_map/ppermute | solution.py:417
  55.6 0.9 %copy-start.2 = (f32[4,64,128]{2,1,0:T(8,128)S(1)}, f32[4,64,128]{2,1,0:T(8,128)}, u32[]{:S(2)}) copy-start(f32[4,64,128]{2,1,0:T(8,128)} %get-tuple-element.34.rest_0_) | copy-start | bytes 393220
  58.9 14.5 %copy-start.5 = (f32[1,64,4096]{2,1,0:T(8,128)S(1)}, f32[1,64,4096]{2,1,0:T(8,128)}, u32[]{:S(2)}) copy-start(f32[1,64,4096]{2,1,0:T(8,128)} %param.10) | copy-start | bytes 3145732

commit v2 on v1

--- a/solution.py
+++ b/solution.py
@@ -164,46 +164,84 @@
     )(owners, *blocks)
 
 
-def spread_kernel(count, slots, pieces, steps, owner_ref, power_ref, science_ref, *rest):
+def early_kernel(count, slots, pieces, steps, owner_ref, power_ref, science_ref, *rest):
     blocks = rest[: len(steps)]
-    out_ref, place, seen, held, sems = rest[-5:]
+    out_ref, place, seen = rest[len(steps) :]
     me = lax.axis_index("visit")
     power = power_ref[0]
     find_places(count, slots, pieces, me, owner_ref, place, seen)
-    for stage in range(2):
-        for number, position, slot, k in each_slot(count, slots, me, place, steps):
-
-            def go(number=number, position=position, slot=slot, k=k, stage=stage):
-                store = pltpu.make_async_copy(held.at[number], out_ref.at[:, at_piece(k)], sems.at[number])
-                if stage == 0:
-                    held[number] = science_ref[:, at_piece(k)] + power * blocks[position][slot]
-                    store.start()
-                else:
-                    store.wait()
-
-            when_taken(count, slots, pieces, k, go)
-
-
-def spread(owners, power, science_var, blocks, steps, count, partial=None):
+    for _, position, slot, k in each_slot(count, slots, me, place, steps):
+
+        def put(position=position, slot=slot, k=k):
+            out_ref[:, at_piece(k)] = science_ref[:, at_piece(k)] + power * blocks[position][slot]
+
+        when_taken(count, slots, pieces, k, put)
+
+
+def early_spread(owners, power, science_var, blocks, steps, count):
+    pieces = owners.shape[1]
+    slots, rows = blocks[0].shape[:2]
+    size = slots * len(steps) * rows * PIECE
+    return pl.pallas_call(
+        functools.partial(early_kernel, count, slots, pieces, steps),
+        out_shape=jax.ShapeDtypeStruct(science_var.shape, jnp.float32),
+        in_specs=[pl.BlockSpec(memory_space=SMEM)] * 2 + [pl.BlockSpec(memory_space=VMEM)] * (1 + len(steps)),
+        out_specs=pl.BlockSpec(memory_space=VMEM),
+        scratch_shapes=places_scratch(count, slots),
+        cost_estimate=pl.CostEstimate(flops=2 * size, transcendentals=0, bytes_accessed=3 * size * 4),
+        compiler_params=pltpu.CompilerParams(vmem_limit_bytes=6 << 20),
+        name="early",
+    )(owners, power, science_var, *blocks)
+
+
+def late_kernel(count, slots, pieces, first, steps, owner_ref, power_ref, science_ref, early_ref, *rest):
+    blocks = rest[: len(steps)]
+    out_ref, place, seen, held, early_sems, sems = rest[len(steps) :]
+    me = lax.axis_index("visit")
+    power = power_ref[0]
+    find_places(count, slots, pieces, me, owner_ref, place, seen)
+
+    def store_early(number, k):
+        return pltpu.make_async_copy(early_ref.at[:, at_piece(k)], out_ref.at[:, at_piece(k)], early_sems.at[number])
+
+    def store_late(number, k):
+        return pltpu.make_async_copy(held.at[number], out_ref.at[:, at_piece(k)], sems.at[number])
+
+    for number, _, _, k in each_slot(count, slots, me, place, first):
+        when_taken(count, slots, pieces, k, lambda number=number, k=k: store_early(number, k).start())
+    for number, position, slot, k in each_slot(count, slots, me, place, steps):
+
+        def put(number=number, position=position, slot=slot, k=k):
+            held[number] = science_ref[:, at_piece(k)] + power * blocks[position][slot]
+            store_late(number, k).start()
+
+        when_taken(count, slots, pieces, k, put)
+    for number, _, _, k in each_slot(count, slots, me, place, first):
+        when_taken(count, slots, pieces, k, lambda number=number, k=k: store_early(number, k).wait())
+    for number, _, _, k in each_slot(count, slots, me, place, steps):
+        when_taken(count, slots, pieces, k, lambda number=number, k=k: store_late(number, k).wait())
+
+
+def late_spread(owners, power, science_var, early, blocks, first, steps, count):
     pieces = owners.shape[1]
     slots, rows = blocks[0].shape[:2]
     number = slots * len(steps)
     size = number * rows * PIECE
-    before = [] if partial is None else [partial]
-    return pl.pallas_call(
-        functools.partial(spread_kernel, count, slots, pieces, steps),
+    return pl.pallas_call(
+        functools.partial(late_kernel, count, slots, pieces, first, steps),
         out_shape=jax.ShapeDtypeStruct(science_var.shape, jnp.float32),
-        in_specs=[pl.BlockSpec(memory_space=SMEM)] * 2
-        + [pl.BlockSpec(memory_space=VMEM)] * (1 + len(steps))
-        + [pl.BlockSpec(memory_space=pl.ANY)] * len(before),
+        in_specs=[pl.BlockSpec(memory_space=SMEM)] * 2 + [pl.BlockSpec(memory_space=VMEM)] * (2 + len(steps)),
         out_specs=pl.BlockSpec(memory_space=pl.ANY),
-        input_output_aliases={3 + len(steps): 0} if before else {},
         scratch_shapes=places_scratch(count, slots)
-        + [pltpu.VMEM((number, rows, PIECE), jnp.float32), pltpu.SemaphoreType.DMA((number,))],
-        cost_estimate=pl.CostEstimate(flops=2 * size, transcendentals=0, bytes_accessed=3 * size * 4),
+        + [
+            pltpu.VMEM((number, rows, PIECE), jnp.float32),
+            pltpu.SemaphoreType.DMA((slots * len(first),)),
+            pltpu.SemaphoreType.DMA((number,)),
+        ],
+        cost_estimate=pl.CostEstimate(flops=2 * size, transcendentals=0, bytes_accessed=4 * size * 4),
         compiler_params=pltpu.CompilerParams(vmem_limit_bytes=6 << 20),
-        name="spread",
-    )(owners, power, science_var, *blocks, *before)
+        name="late",
+    )(owners, power, science_var, early, *blocks)
 
 
 def split(x):
@@ -426,14 +464,13 @@
     tiles = lax.axis_size("tile")
     above = lax.ppermute(tail, "tile", [(i, i + 1) for i in range(tiles - 1)])
     below = lax.ppermute(head, "tile", [(i + 1, i) for i in range(tiles - 1)])
-    first = [0] + near_steps(count)
+    first, second = [0] + near_steps(count), far_steps(count)
     blocks = [got_var[step] for step in first]
-    difference_var = spread(owners, power, science_var[0], blocks, first, count)
+    early = early_spread(owners, power, science_var[0], blocks, first, count)
     shifts = -(-side // GROUP)
     difference = match(margin, shifts, owners, both, above, below, science[0], got)
-    second = far_steps(count)
     blocks = [got_var[step] for step in second]
-    difference_var = spread(owners, power, science_var[0], blocks, second, count, difference_var)
+    difference_var = late_spread(owners, power, science_var[0], early, blocks, first, second, count)
     return difference[None], difference_var[None]
 
 
@@ -447,7 +484,7 @@
 
 def flux_steps(count):
     far = far_steps(count)
-    return far[-1:] + near_steps(count) + far[1:-1] + far[:1]
+    return near_steps(count) + far
 
 
 def solution(mesh):

time: 82.7 us -> 81.3 us (0.983)
  the two profiles are of different devices: /device:TPU:18 before, /device:TPU:11 now
where the time goes in v2:
time: 81.3 us; the launch traced here: 81 us
  waiting for transfers between devices  32.6 us (40%)
  starting transfers between devices  21.2 us (26%)
  Pallas kernels  20.6 us (25%)
  local copies, waits for them, and re-layouts  2.85 us (4%)
  between operations  2.73 us (3%)
  matrix products  0.94 us (1%)
    ppermute x7, waiting for transfers between devices, local(): got[step] = lax.ppermute(mine[step], 'visit', pairs(step, count))  16.9 us
    ppermute x7, waiting for transfers between devices, local(): got_var[step] = lax.ppermute(mine_var[step], 'visit', pairs(step, count))  15.7 us
    pallas_call x1, Pallas kernels, match(): pl.pallas_call(functools.partial(match_kernel, margin, shifts, count, slo...  8.95 us
    ppermute x7, starting transfers between devices, local(): got_var[step] = lax.ppermute(mine_var[step], 'visit', pairs(step, count))  7.66 us
    ppermute x7, starting transfers between devices, local(): got[step] = lax.ppermute(mine[step], 'visit', pairs(step, count))  7.45 us
    pallas_call x2, Pallas kernels, cut(): pl.pallas_call(functools.partial(cut_kernel, count, slots, owners.shape[1...  5.68 us
    ppermute x1, starting transfers between devices, local(): below = lax.ppermute(head, 'tile', [(i + 1, i) for i in range(tiles - 1)])  4.84 us
    pallas_call x1, Pallas kernels, late_spread(): pl.pallas_call(functools.partial(late_kernel, count, slots, pieces, first...  2.63 us
  transfers between devices with their start and end apart: 16, of which 9 were waited for; matrix products, arithmetic and copies ran while one was open for 4% of the time, Pallas kernels for 11%

profile of v2, /device:TPU:11, one launch (start us, length us, event | category | flops | bytes accessed | tf_op | source)
XLA Modules:
  0.0 81.0 jit_solution(8713606260747863668)
XLA Ops:
  0.6 2.8 %cut.2 = (f32[4,64,128]{2,1,0:T(8,128)}, f32[4,64,128]{2,1,0:T(8,128)}, f32[4,64,128]{2,1,0:T(8,128)}, f32[4,64,128]{2,1,0:T(8,128)}, f32[4,64,128]{2,1,0:T(8,12...) custom-call(s32[8,32]{1,0:T(8,128)} %bitcast.15, s32[8,32]{1,0:T(8,128)} %offset_hbm.3, ...), custom_call_target="tpu_custom_call" | custom-call | bytes 2097152 | tf_op jit(solution)/shard_map/cut/pallas_call | solution.py:79
  3.4 1.3 %collective-permute-start = (f32[4,64,128]{2,1,0:T(8,128)}, f32[4,64,128]{2,1,0:T(8,128)S(1)}, u32[]{:S(2)}, u32[]{:S(2)}) collective-permute-start(f32[4,64,128]{2,1,0:T(8,128)} %get-tuple-element.21), channel_id=1, source_target_pairs={{0,4},{4,0},{8,12},{12,8},{16,20},{20,16},{24,28},{28,24},{1,5},{5... | collective-permute-start | bytes 393224 | tf_op jit(solution)/shard_map/ppermute | solution.py:451
  4.9 1.2 %collective-permute-start.2 = (f32[4,64,128]{2,1,0:T(8,128)}, f32[4,64,128]{2,1,0:T(8,128)S(1)}, u32[]{:S(2)}, u32[]{:S(2)}) collective-permute-start(f32[4,64,128]{2,1,0:T(8,128)} %get-tuple-element.23), channel_id=1, source_target_pairs={{0,12},{4,8},{8,4},{12,0},{16,28},{20,24},{24,20},{28,16},{1,13},{... | collective-permute-start | bytes 393224 | tf_op jit(solution)/shard_map/ppermute | solution.py:451
  6.1 2.3 %collective-permute-start.3 = (f32[4,64,128]{2,1,0:T(8,128)}, f32[4,64,128]{2,1,0:T(8,128)S(1)}, u32[]{:S(2)}, u32[]{:S(2)}) collective-permute-start(f32[4,64,128]{2,1,0:T(8,128)} %get-tuple-element.24), channel_id=1, source_target_pairs={{0,16},{4,20},{8,24},{12,28},{16,0},{20,4},{24,8},{28,12},{1,17},{... | collective-permute-start | bytes 393224 | tf_op jit(solution)/shard_map/ppermute | solution.py:451
  9.4 1.3 %collective-permute-start.5 = (f32[4,64,128]{2,1,0:T(8,128)}, f32[4,64,128]{2,1,0:T(8,128)S(1)}, u32[]{:S(2)}, u32[]{:S(2)}) collective-permute-start(f32[4,64,128]{2,1,0:T(8,128)} %get-tuple-element.26), channel_id=1, source_target_pairs={{0,24},{4,28},{8,16},{12,20},{16,8},{20,12},{24,0},{28,4},{1,25},{... | collective-permute-start | bytes 393224 | tf_op jit(solution)/shard_map/ppermute | solution.py:451
  10.9 2.9 %cut.3 = (f32[4,64,128]{2,1,0:T(8,128)}, f32[4,64,128]{2,1,0:T(8,128)}, f32[4,64,128]{2,1,0:T(8,128)}, f32[4,64,128]{2,1,0:T(8,128)}, f32[4,64,128]{2,1,0:T(8,12...) custom-call(s32[8,32]{1,0:T(8,128)} %bitcast.16, s32[8,32]{1,0:T(8,128)} %offset_hbm.3, ...), custom_call_target="tpu_custom_call" | custom-call | bytes 2097152 | tf_op jit(solution)/shard_map/cut/pallas_call | solution.py:79
  14.0 1.1 %collective-permute-start.9 = (f32[4,64,128]{2,1,0:T(8,128)}, f32[4,64,128]{2,1,0:T(8,128)S(1)}, u32[]{:S(2)}, u32[]{:S(2)}) collective-permute-start(f32[4,64,128]{2,1,0:T(8,128)} %get-tuple-element.31), channel_id=1, source_target_pairs={{0,4},{4,0},{8,12},{12,8},{16,20},{20,16},{24,28},{28,24},{1,5},{5... | collective-permute-start | bytes 393224 | tf_op jit(solution)/shard_map/ppermute | solution.py:455
  15.4 8.9 %collective-permute-done.4.rest_5_ = f32[4,64,128]{2,1,0:T(8,128)S(1)} collective-permute-done((f32[4,64,128]{2,1,0:T(8,128)}, f32[4,64,128]{2,1,0:T(8,128)S(1)}, u32[]{:S(2)}, u32[]{:S(2)}) %collective-permute-start.4) | collective-permute-done | bytes 131104 | tf_op jit(solution)/shard_map/ppermute | solution.py:451
  24.2 3.7 %collective-permute-done.5.rest_6_ = f32[4,64,128]{2,1,0:T(8,128)S(1)} collective-permute-done((f32[4,64,128]{2,1,0:T(8,128)}, f32[4,64,128]{2,1,0:T(8,128)S(1)}, u32[]{:S(2)}, u32[]{:S(2)}) %collective-permute-start.5) | collective-permute-done | bytes 131104 | tf_op jit(solution)/shard_map/ppermute | solution.py:451
  27.9 3.9 %collective-permute-done.6.rest_7_ = f32[4,64,128]{2,1,0:T(8,128)S(1)} collective-permute-done((f32[4,64,128]{2,1,0:T(8,128)}, f32[4,64,128]{2,1,0:T(8,128)S(1)}, u32[]{:S(2)}, u32[]{:S(2)}) %collective-permute-start.6) | collective-permute-done | bytes 131104 | tf_op jit(solution)/shard_map/ppermute | solution.py:451
  31.8 1.8 %edges.1 = (f32[24,4096]{1,0:T(8,128)}, f32[24,4096]{1,0:T(8,128)}) custom-call(s32[8,32]{1,0:T(8,128)S(1)} %bitcast.17, f32[4,64,128]{2,1,0:T(8,128)S(1)} %copy-done.3, f32[4,64,128]{2,1,0:T(8,128)S(1)} %collective-permute-done.rest_1_, f32[4,64,128]{2,1,0:T(8,128)S(1)} %collective-permute-done.1.rest_2_, f32[4,64,128]{2,1,0:T(8,128)S(1)} %collective-permute-done.2.rest_3_, ...), custom_call_target="tpu_custom_call" | custom-call | bytes 1572864 | tf_op jit(solution)/shard_map/edges/pallas_call | solution.py:155
  33.6 1.3 %collective-permute-start.7 = (f32[24,4096]{1,0:T(8,128)}, f32[24,4096]{1,0:T(8,128)}, u32[]{:S(2)}, u32[]{:S(2)}) collective-permute-start(f32[24,4096]{1,0:T(8,128)} %get-tuple-element.28), channel_id=1, source_target_pairs={{0,1},{1,2},{2,3},{4,5},{5,6},{6,7},{8,9},{9,10},{10,11},{12,13},{... | collective-permute-start | bytes 1179656 | tf_op jit(solution)/shard_map/ppermute | solution.py:465
  34.9 4.8 %collective-permute-start.8 = (f32[24,4096]{1,0:T(8,128)}, f32[24,4096]{1,0:T(8,128)}, u32[]{:S(2)}, u32[]{:S(2)}) collective-permute-start(f32[24,4096]{1,0:T(8,128)} %get-tuple-element.29), channel_id=1, source_target_pairs={{1,0},{2,1},{3,2},{5,4},{6,5},{7,6},{9,8},{10,9},{11,10},{13,12},{... | collective-permute-start | bytes 1179656 | tf_op jit(solution)/shard_map/ppermute | solution.py:466
  39.7 1.4 %collective-permute-start.11 = (f32[4,64,128]{2,1,0:T(8,128)}, f32[4,64,128]{2,1,0:T(8,128)S(1)}, u32[]{:S(2)}, u32[]{:S(2)}) collective-permute-start(f32[4,64,128]{2,1,0:T(8,128)} %get-tuple-element.33), channel_id=1, source_target_pairs={{0,12},{4,8},{8,4},{12,0},{16,28},{20,24},{24,20},{28,16},{1,13},{... | collective-permute-start | bytes 393224 | tf_op jit(solution)/shard_map/ppermute | solution.py:455
  41.1 1.6 %collective-permute-start.12 = (f32[4,64,128]{2,1,0:T(8,128)}, f32[4,64,128]{2,1,0:T(8,128)S(1)}, u32[]{:S(2)}, u32[]{:S(2)}) collective-permute-start(f32[4,64,128]{2,1,0:T(8,128)} %get-tuple-element.34), channel_id=1, source_target_pairs={{0,16},{4,20},{8,24},{12,28},{16,0},{20,4},{24,8},{28,12},{1,17},{... | collective-permute-start | bytes 393224 | tf_op jit(solution)/shard_map/ppermute | solution.py:455
  42.7 1.3 %dynamic_slice.7 = s32[1,1]{0,1:T(1,128)} dynamic-slice(s32[8,4]{0,1:T(4,128)} %param.19, s32[]{:T(128)S(6)} %select_n.10, s32[]{:T(128)S(6)} %select_n.11), dynamic_slice_sizes={1,1} | dynamic-slice | bytes 12 | tf_op jit(solution)/shard_map/dynamic_slice | solution.py:457
  46.6 1.7 %collective-permute-start.13 = (f32[4,64,128]{2,1,0:T(8,128)}, f32[4,64,128]{2,1,0:T(8,128)S(1)}, u32[]{:S(2)}, u32[]{:S(2)}) collective-permute-start(f32[4,64,128]{2,1,0:T(8,128)} %get-tuple-element.35), channel_id=1, source_target_pairs={{0,20},{4,16},{8,28},{12,24},{16,4},{20,0},{24,12},{28,8},{1,21},{... | collective-permute-start | bytes 393224 | tf_op jit(solution)/shard_map/ppermute | solution.py:455
  48.4 1.8 %collective-permute-start.14 = (f32[4,64,128]{2,1,0:T(8,128)}, f32[4,64,128]{2,1,0:T(8,128)S(1)}, u32[]{:S(2)}, u32[]{:S(2)}) collective-permute-start(f32[4,64,128]{2,1,0:T(8,128)} %get-tuple-element.36), channel_id=1, source_target_pairs={{0,24},{4,28},{8,16},{12,20},{16,8},{20,12},{24,0},{28,4},{1,25},{... | collective-permute-start | bytes 393224 | tf_op jit(solution)/shard_map/ppermute | solution.py:455
  52.8 1.5 %early.1.early_ref = f32[64,4096]{1,0:T(8,128)S(1)} custom-call(s32[8,32]{1,0:T(8,128)S(1)} %bitcast.18, f32[1]{0:T(128)} %bitcast.7.power_ref, f32[64,4096]{1,0:T(8,128)S(1)} %bitcast.13, f32[4,64,128]{2,1,0:T(8,128)S(1)} %copy-done.2, f32[4,64,128]{2,1,0:T(8,128)S(1)} %collective-permute-done.9.rest_1_, f32[4,64,128]{2,1,0:T(8,128)S(1)} %collective-permute-done.10.rest_2_, ...), custom_call_target="tpu_custom_call" | custom-call | flops 262144 | bytes 1572864 | tf_op jit(solution)/shard_map/early/pallas_call | solution.py:185
  54.3 7.0 %collective-permute-done.13.rest_1_ = f32[4,64,128]{2,1,0:T(8,128)S(1)} collective-permute-done((f32[4,64,128]{2,1,0:T(8,128)}, f32[4,64,128]{2,1,0:T(8,128)S(1)}, u32[]{:S(2)}, u32[]{:S(2)}) %collective-permute-start.13) | collective-permute-done | bytes 131104 | tf_op jit(solution)/shard_map/ppermute | solution.py:455
  61.3 5.2 %collective-permute-done.14.rest_2_ = f32[4,64,128]{2,1,0:T(8,128)S(1)} collective-permute-done((f32[4,64,128]{2,1,0:T(8,128)}, f32[4,64,128]{2,1,0:T(8,128)S(1)}, u32[]{:S(2)}, u32[]{:S(2)}) %collective-permute-start.14) | collective-permute-done | bytes 131104 | tf_op jit(solution)/shard_map/ppermute | solution.py:455
  66.5 2.8 %collective-permute-done.15.rest_3_ = f32[4,64,128]{2,1,0:T(8,128)S(1)} collective-permute-done((f32[4,64,128]{2,1,0:T(8,128)}, f32[4,64,128]{2,1,0:T(8,128)S(1)}, u32[]{:S(2)}, u32[]{:S(2)}) %collective-permute-start.15) | collective-permute-done | bytes 131104 | tf_op jit(solution)/shard_map/ppermute | solution.py:455
  69.3 2.6 %late.1 = f32[64,4096]{1,0:T(8,128)} custom-call(s32[8,32]{1,0:T(8,128)S(1)} %bitcast.19, f32[1]{0:T(128)} %bitcast.7.power_ref, f32[64,4096]{1,0:T(8,128)S(1)} %bitcast.14, f32[64,4096]{1,0:T(8,128)S(1)} %early.1.early_ref, f32[4,64,128]{2,1,0:T(8,128)S(1)} %collective-permute-done.12.rest_0_, f32[4,64,128]{2,1,0:T(8,128)S(1)} %collective-permute-done.13.rest_1_, ...), custom_call_target="tpu_custom_call" | custom-call | flops 262144 | bytes 2097152 | tf_op jit(solution)/shard_map/late/pallas_call | solution.py:230
  72.0 9.0 %match.1 = f32[64,4096]{1,0:T(8,128)} custom-call(s32[8,32]{1,0:T(8,128)S(1)} %bitcast.20, bf16[352,256]{1,0:T(8,128)(2,1)S(1)} %bands.1.both_ref, f32[24,4096]{1,0:T(8,128)} %collective-permute-done.7.above_ref, f32[24,4096]{1,0:T(8,128)} %collective-permute-done.8.below_ref, f32[64,4096]{1,0:T(8,128)S(1)} %bitcast.21, f32[4,64,128]{2,1,0:T(8,128)S(1)} %copy-done.3, ...), custom_call_target="tpu_custom_call" | custom-call | flops 4429185024 | bytes 4194304 | tf_op jit(solution)/shard_map/match/pallas_call | solution.py:401
  (36 shorter events, 5.0 us)
Async XLA Ops:
  0.6 50.2 %copy-start = (f32[16,41]{1,0:T(8,128)S(1)}, f32[16,41]{1,0:T(8,128)}, u32[]{:S(2)}) copy-start(f32[16,41]{1,0:T(8,128)} %param.16) | copy-start | bytes 7876
  3.4 6.0 %collective-permute-start = (f32[4,64,128]{2,1,0:T(8,128)}, f32[4,64,128]{2,1,0:T(8,128)S(1)}, u32[]{:S(2)}, u32[]{:S(2)}) collective-permute-start(f32[4,64,128]{2,1,0:T(8,128)} %get-tuple-element.21), channel_id=1, source_target_pairs={{0,4},{4,0},{8,12},{12,8},{16,20},{20,16},{24,28},{28,24},{1,5},{5... | collective-permute-start | bytes 393224 | tf_op jit(solution)/shard_map/ppermute | solution.py:451
  4.7 6.0 %collective-permute-start.1 = (f32[4,64,128]{2,1,0:T(8,128)}, f32[4,64,128]{2,1,0:T(8,128)S(1)}, u32[]{:S(2)}, u32[]{:S(2)}) collective-permute-start(f32[4,64,128]{2,1,0:T(8,128)} %get-tuple-element.22), channel_id=1, source_target_pairs={{0,8},{4,12},{8,0},{12,4},{16,24},{20,28},{24,16},{28,20},{1,9},{5... | collective-permute-start | bytes 393224 | tf_op jit(solution)/shard_map/ppermute | solution.py:451
  4.9 9.1 %collective-permute-start.2 = (f32[4,64,128]{2,1,0:T(8,128)}, f32[4,64,128]{2,1,0:T(8,128)S(1)}, u32[]{:S(2)}, u32[]{:S(2)}) collective-permute-start(f32[4,64,128]{2,1,0:T(8,128)} %get-tuple-element.23), channel_id=1, source_target_pairs={{0,12},{4,8},{8,4},{12,0},{16,28},{20,24},{24,20},{28,16},{1,13},{... | collective-permute-start | bytes 393224 | tf_op jit(solution)/shard_map/ppermute | solution.py:451
  6.1 9.2 %collective-permute-start.3 = (f32[4,64,128]{2,1,0:T(8,128)}, f32[4,64,128]{2,1,0:T(8,128)S(1)}, u32[]{:S(2)}, u32[]{:S(2)}) collective-permute-start(f32[4,64,128]{2,1,0:T(8,128)} %get-tuple-element.24), channel_id=1, source_target_pairs={{0,16},{4,20},{8,24},{12,28},{16,0},{20,4},{24,8},{28,12},{1,17},{... | collective-permute-start | bytes 393224 | tf_op jit(solution)/shard_map/ppermute | solution.py:451
  8.4 15.8 %collective-permute-start.4 = (f32[4,64,128]{2,1,0:T(8,128)}, f32[4,64,128]{2,1,0:T(8,128)S(1)}, u32[]{:S(2)}, u32[]{:S(2)}) collective-permute-start(f32[4,64,128]{2,1,0:T(8,128)} %get-tuple-element.25), channel_id=1, source_target_pairs={{0,20},{4,16},{8,28},{12,24},{16,4},{20,0},{24,12},{28,8},{1,21},{... | collective-permute-start | bytes 393224 | tf_op jit(solution)/shard_map/ppermute | solution.py:451
  9.4 18.5 %collective-permute-start.5 = (f32[4,64,128]{2,1,0:T(8,128)}, f32[4,64,128]{2,1,0:T(8,128)S(1)}, u32[]{:S(2)}, u32[]{:S(2)}) collective-permute-start(f32[4,64,128]{2,1,0:T(8,128)} %get-tuple-element.26), channel_id=1, source_target_pairs={{0,24},{4,28},{8,16},{12,20},{16,8},{20,12},{24,0},{28,4},{1,25},{... | collective-permute-start | bytes 393224 | tf_op jit(solution)/shard_map/ppermute | solution.py:451
  10.7 21.1 %collective-permute-start.6 = (f32[4,64,128]{2,1,0:T(8,128)}, f32[4,64,128]{2,1,0:T(8,128)S(1)}, u32[]{:S(2)}, u32[]{:S(2)}) collective-permute-start(f32[4,64,128]{2,1,0:T(8,128)} %get-tuple-element.27), channel_id=1, source_target_pairs={{0,28},{4,24},{8,20},{12,16},{16,12},{20,8},{24,4},{28,0},{1,29},{... | collective-permute-start | bytes 393224 | tf_op jit(solution)/shard_map/ppermute | solution.py:451
  10.9 21.0 %copy-start.3 = (f32[4,64,128]{2,1,0:T(8,128)S(1)}, f32[4,64,128]{2,1,0:T(8,128)}, u32[]{:S(2)}) copy-start(f32[4,64,128]{2,1,0:T(8,128)} %get-tuple-element.20.rest_0_) | copy-start | bytes 393220
  10.9 21.0 %copy-start.4 = (s32[8,32,1]{1,2,0:T(1,128)S(1)}, s32[8,32,1]{1,2,0:T(1,128)}, u32[]{:S(2)}) copy-start(s32[8,32,1]{1,2,0:T(1,128)} %param.14) | copy-start | bytes 3076
  13.8 38.3 %copy-start.1 = (f32[1,64,4096]{2,1,0:T(8,128)S(1)}, f32[1,64,4096]{2,1,0:T(8,128)}, u32[]{:S(2)}) copy-start(f32[1,64,4096]{2,1,0:T(8,128)} %param.11) | copy-start | bytes 3145732
  14.0 27.1 %collective-permute-start.9 = (f32[4,64,128]{2,1,0:T(8,128)}, f32[4,64,128]{2,1,0:T(8,128)S(1)}, u32[]{:S(2)}, u32[]{:S(2)}) collective-permute-start(f32[4,64,128]{2,1,0:T(8,128)} %get-tuple-element.31), channel_id=1, source_target_pairs={{0,4},{4,0},{8,12},{12,8},{16,20},{20,16},{24,28},{28,24},{1,5},{5... | collective-permute-start | bytes 393224 | tf_op jit(solution)/shard_map/ppermute | solution.py:455
  33.6 38.4 %collective-permute-start.7 = (f32[24,4096]{1,0:T(8,128)}, f32[24,4096]{1,0:T(8,128)}, u32[]{:S(2)}, u32[]{:S(2)}) collective-permute-start(f32[24,4096]{1,0:T(8,128)} %get-tuple-element.28), channel_id=1, source_target_pairs={{0,1},{1,2},{2,3},{4,5},{5,6},{6,7},{8,9},{9,10},{10,11},{12,13},{... | collective-permute-start | bytes 1179656 | tf_op jit(solution)/shard_map/ppermute | solution.py:465
  34.9 37.1 %collective-permute-start.8 = (f32[24,4096]{1,0:T(8,128)}, f32[24,4096]{1,0:T(8,128)}, u32[]{:S(2)}, u32[]{:S(2)}) collective-permute-start(f32[24,4096]{1,0:T(8,128)} %get-tuple-element.29), channel_id=1, source_target_pairs={{1,0},{2,1},{3,2},{5,4},{6,5},{7,6},{9,8},{10,9},{11,10},{13,12},{... | collective-permute-start | bytes 1179656 | tf_op jit(solution)/shard_map/ppermute | solution.py:466
  39.7 6.9 %collective-permute-start.10 = (f32[4,64,128]{2,1,0:T(8,128)}, f32[4,64,128]{2,1,0:T(8,128)S(1)}, u32[]{:S(2)}, u32[]{:S(2)}) collective-permute-start(f32[4,64,128]{2,1,0:T(8,128)} %get-tuple-element.32), channel_id=1, source_target_pairs={{0,8},{4,12},{8,0},{12,4},{16,24},{20,28},{24,16},{28,20},{1,9},{5... | collective-permute-start | bytes 393224 | tf_op jit(solution)/shard_map/ppermute | solution.py:455
  39.7 8.7 %collective-permute-start.11 = (f32[4,64,128]{2,1,0:T(8,128)}, f32[4,64,128]{2,1,0:T(8,128)S(1)}, u32[]{:S(2)}, u32[]{:S(2)}) collective-permute-start(f32[4,64,128]{2,1,0:T(8,128)} %get-tuple-element.33), channel_id=1, source_target_pairs={{0,12},{4,8},{8,4},{12,0},{16,28},{20,24},{24,20},{28,16},{1,13},{... | collective-permute-start | bytes 393224 | tf_op jit(solution)/shard_map/ppermute | solution.py:455
  41.1 9.7 %collective-permute-start.12 = (f32[4,64,128]{2,1,0:T(8,128)}, f32[4,64,128]{2,1,0:T(8,128)S(1)}, u32[]{:S(2)}, u32[]{:S(2)}) collective-permute-start(f32[4,64,128]{2,1,0:T(8,128)} %get-tuple-element.34), channel_id=1, source_target_pairs={{0,16},{4,20},{8,24},{12,28},{16,0},{20,4},{24,8},{28,12},{1,17},{... | collective-permute-start | bytes 393224 | tf_op jit(solution)/shard_map/ppermute | solution.py:455
  44.0 6.8 %copy-start.6 = (f32[16,41]{1,0:T(8,128)S(1)}, f32[16,41]{1,0:T(8,128)}, u32[]{:S(2)}) copy-start(f32[16,41]{1,0:T(8,128)} %param.17) | copy-start | bytes 7876
  46.6 14.7 %collective-permute-start.13 = (f32[4,64,128]{2,1,0:T(8,128)}, f32[4,64,128]{2,1,0:T(8,128)S(1)}, u32[]{:S(2)}, u32[]{:S(2)}) collective-permute-start(f32[4,64,128]{2,1,0:T(8,128)} %get-tuple-element.35), channel_id=1, source_target_pairs={{0,20},{4,16},{8,28},{12,24},{16,4},{20,0},{24,12},{28,8},{1,21},{... | collective-permute-start | bytes 393224 | tf_op jit(solution)/shard_map/ppermute | solution.py:455
  48.4 18.2 %collective-permute-start.14 = (f32[4,64,128]{2,1,0:T(8,128)}, f32[4,64,128]{2,1,0:T(8,128)S(1)}, u32[]{:S(2)}, u32[]{:S(2)}) collective-permute-start(f32[4,64,128]{2,1,0:T(8,128)} %get-tuple-element.36), channel_id=1, source_target_pairs={{0,24},{4,28},{8,16},{12,20},{16,8},{20,12},{24,0},{28,4},{1,25},{... | collective-permute-start | bytes 393224 | tf_op jit(solution)/shard_map/ppermute | solution.py:455
  50.8 18.5 %collective-permute-start.15 = (f32[4,64,128]{2,1,0:T(8,128)}, f32[4,64,128]{2,1,0:T(8,128)S(1)}, u32[]{:S(2)}, u32[]{:S(2)}) collective-permute-start(f32[4,64,128]{2,1,0:T(8,128)} %get-tuple-element.37), channel_id=1, source_target_pairs={{0,28},{4,24},{8,20},{12,16},{16,12},{20,8},{24,4},{28,0},{1,29},{... | collective-permute-start | bytes 393224 | tf_op jit(solution)/shard_map/ppermute | solution.py:455
  51.8 0.9 %copy-start.2 = (f32[4,64,128]{2,1,0:T(8,128)S(1)}, f32[4,64,128]{2,1,0:T(8,128)}, u32[]{:S(2)}) copy-start(f32[4,64,128]{2,1,0:T(8,128)} %get-tuple-element.30.rest_0_) | copy-start | bytes 393220
  54.3 17.7 %copy-start.5 = (f32[1,64,4096]{2,1,0:T(8,128)S(1)}, f32[1,64,4096]{2,1,0:T(8,128)}, u32[]{:S(2)}) copy-start(f32[1,64,4096]{2,1,0:T(8,128)} %param.10) | copy-start | bytes 3145732
